TPU v7x, 32 devices: a whole 2x2x4 slice. The times are simulated.
32 devices in a mesh: dp: 8 (over y, x, core), expert: 4 (over z).
Axes of the slice: x: 2, y: 2, z: 4, core: 2. Of those that a mesh axis runs over, the one named last changes fastest.
Arguments:
- tokens: bfloat16 [4096, 1280], P(('dp', 'expert')), may hold values from -6 to 6
- cotangent: bfloat16 [4096, 1280], P(('dp', 'expert')), may hold values from -4 to 4
- gate_weights: float32 [4096, 2], P(('dp', 'expert')), may hold values from 0.1 to 1
- expert_ids: int32 [4096, 2], P(('dp', 'expert')), may hold values from 0 to 7, as said below
- segments: int32 [32, 128], P(('dp', 'expert')), may hold values from 0 to 3, never falling along the last dimension, each value on 1 to 64 neighbouring positions
- keep_counts: int32 [32, 4], P(('dp', 'expert')), may hold values from 1 to 64
- expand_weight: bfloat16 [8, 2560, 1280], P('expert', 'dp'), may hold values from -0.15625 to 0.15625
- reduce_weight: bfloat16 [8, 2560, 1280], P('expert', 'dp'), may hold values from -0.125 to 0.125
Outputs:
- output: bfloat16 [4096, 1280], P(('dp', 'expert'))
- tokens_grad: bfloat16 [4096, 1280], P(('dp', 'expert'))
- gating_grad: float32 [4096, 2], P(('dp', 'expert'))
- expand_grad: bfloat16 [8, 2560, 1280], P('expert', 'dp')
- reduce_grad: bfloat16 [8, 2560, 1280], P('expert', 'dp')
Inputs may be any that keep to these rules, and one draw needn't show every extreme that they name: `expert_ids`: the 128 tokens of one sequence name each expert exactly 32 times, and a token's 2 experts differ. `segments`: within a sequence the ids never fall, every image 0 to 3 appears, each holds 1 to 64 positions.
All inputs are finite; a program needn't handle non-finite values.
Results may differ from a plain program's by a relative error of at most 0.015.
Values may be sent and summed in bfloat16 or wider, within the bound.
No kernel may reach another device: no remote copies, remote signals or barrier semaphores. Data moves between devices by JAX's collectives and lax.ppermute only.
A program may use at most 128 MiB of HBM per device.

v0:
```python
import functools

import jax
import jax.numpy as jnp
from jax import lax
from jax.experimental import pallas as pl
from jax.experimental.pallas import tpu as pltpu
from jax.sharding import PartitionSpec as P

epsilon = 1e-06
root_half = 0.7071067811865476
density_scale = 0.3989422804014327

split_inputs = False
split_results = False
split_grads = False
merge_near = False
merge_features = False
merge_grads = False
turns = {
    "d0": 0,
    "d1": 1,
    "g0": 0,
    "g1": 1,
    "pd": 0,
    "pg": 1,
    "px": 0,
    "py": 1,
    "x0": 0,
    "x1": 1,
    "y0": 0,
    "y1": 1,
}


def dot(left, right, left_dim, right_dim):
    return lax.dot_general(
        left, right, (((left_dim,), (right_dim,)), ((), ())), preferred_element_type=jnp.float32
    )


def normalize(tokens):
    wide = tokens.astype(jnp.float32)
    centred = wide - jnp.mean(wide, axis=1, keepdims=True)
    inv_scale = lax.rsqrt(jnp.mean(centred * centred, axis=1, keepdims=True) + epsilon)
    return centred * inv_scale, inv_scale


def one_hot(target, rows):
    lanes = lax.broadcasted_iota(jnp.int32, (target.shape[0], rows), 1)
    return (target == lanes).astype(jnp.bfloat16)


def to_column(row, same):
    return jnp.sum(jnp.where(same, row, 0.0), axis=1, keepdims=True)


def scatter_far(refs, values, others, near):
    for number, ref in enumerate(refs):
        index, away = number // others, number % others
        rows = ref.shape[0]
        base = (away + 1) * near + index * rows
        ref[...] = values[base : base + rows]


def route_kernel(
    planes, local, me_ref, *refs
):
    outs, sems = refs[6:-7], refs[-1]
    copies = [
        pltpu.make_async_copy(source, held, sems.at[index])
        for index, (source, held) in enumerate(zip(refs[:6], refs[-7:-1]))
    ]
    for copy in copies:
        copy.start()
    gate_ref, ids_ref, seg_ref, keep_ref, tok_ref, cot_ref = refs[-7:-1]
    *small_copies, tok_copy, cot_copy = copies
    for copy in small_copies:
        copy.wait()
    top, toks = ids_ref.shape
    experts = planes * local
    cap = top * toks // experts
    near_refs = outs[: 1 if merge_near else 2]
    others = planes - 1
    feature_parts = 1 if merge_features else local
    far_refs = outs[len(near_refs) : -3]
    feature_refs, grad_refs = far_refs[: feature_parts * others], far_refs[feature_parts * others :]
    target_ref, weight_ref, alive_ref = outs[-3:]
    seg = seg_ref[...]
    spot = lax.broadcasted_iota(jnp.int32, seg.shape, 1).astype(jnp.float32)
    alive_row = jnp.zeros(seg.shape, jnp.float32)
    for image in range(keep_ref.shape[1]):
        start = jnp.sum((seg < image).astype(jnp.float32), axis=1, keepdims=True)
        limit = keep_ref[0:1, image : image + 1].astype(jnp.float32)
        alive_row = jnp.where((seg == image) & (spot - start < limit), 1.0, alive_row)
    row = lax.broadcasted_iota(jnp.int32, (toks, toks), 0)
    col = lax.broadcasted_iota(jnp.int32, (toks, toks), 1)
    same = row == col
    alive = to_column(alive_row, same)
    width = -(-experts // 128) * 128
    lanes = lax.broadcasted_iota(jnp.int32, (toks, width), 1)
    picks = [
        to_column(ids_ref[k : k + 1, :].astype(jnp.float32), same).astype(jnp.int32)
        for k in range(top)
    ]
    chosen = [(pick == lanes).astype(jnp.float32) for pick in picks]
    every = chosen[0]
    for k in range(1, top):
        every = every + chosen[k]
    before = dot((col < row).astype(jnp.bfloat16), every.astype(jnp.bfloat16), 1, 0)
    me = me_ref[0]
    hots = []
    weights = []
    for k in range(top):
        slot = jnp.sum(before * chosen[k], axis=1, keepdims=True).astype(jnp.int32)
        away = jnp.bitwise_xor(lax.div(picks[k], local), me)
        target = (away * local + lax.rem(picks[k], local)) * cap + slot
        weight = to_column(gate_ref[k : k + 1, :] * alive_row, same)
        target_ref[:, k : k + 1] = target
        weight_ref[:, k : k + 1] = weight
        hots.append(one_hot(target, experts * cap))
        weights.append(weight)
    alive_ref[...] = alive
    tok_copy.wait()
    normed, _ = normalize(tok_ref[...])
    low = jnp.where(alive > 0, normed, 0.0).astype(jnp.bfloat16)
    every_hot = hots[0]
    for k in range(1, top):
        every_hot = every_hot + hots[k]
    features = dot(every_hot, low, 0, 0).astype(jnp.bfloat16)
    near = local * cap
    near_refs[0][:near] = features[:near]
    scatter_far(feature_refs, features, others, near)
    cot_copy.wait()
    cot = cot_ref[...].astype(jnp.float32)
    scaled = [(cot * weight).astype(jnp.bfloat16) for weight in weights]
    grads = dot(jnp.concatenate(hots, 0), jnp.concatenate(scaled, 0), 0, 0).astype(jnp.bfloat16)
    near_refs[-1][near_refs[-1].shape[0] - near :] = grads[:near]
    scatter_far(grad_refs, grads, others, near)


def join_kernel(others, cap, merge, *refs):
    piece_refs, outs = refs[:others], refs[others:]
    for l in range(piece_refs[0].shape[0] // cap):
        out = outs[0 if merge else l]
        base = l * others * cap if merge else 0
        for away, ref in enumerate(piece_refs):
            out[base + away * cap : base + (away + 1) * cap] = ref[l * cap : (l + 1) * cap]


def add_kernel(*refs):
    total = refs[0][0].astype(jnp.float32)
    for ref in refs[1:-1]:
        total = total + ref[0].astype(jnp.float32)
    refs[-1][0] = total.astype(jnp.bfloat16)


def joined(own_refs, other_refs):
    return jnp.concatenate(
        [ref[...] for pair in zip(own_refs, other_refs) for ref in pair], 0
    )


def forward_kernel(blocks, parts, held, *refs):
    rows = joined(refs[:blocks], refs[blocks : 2 * blocks])
    up_own, up_pair, down_own, down_pair = refs[2 * blocks : 2 * blocks + 4]
    held_refs = refs[2 * blocks + 4 : 2 * blocks + 4 + held]
    hidden_ref, slope_ref, *outs = refs[2 * blocks + 4 + held :]
    up = jnp.concatenate([up_own[0], up_pair[0]], 0)
    pre = dot(rows, up, 1, 1)
    half = 0.5 * (1.0 + lax.erf(pre * root_half))
    hidden = (pre * half).astype(jnp.bfloat16)
    hidden_ref[...] = hidden
    slope_ref[...] = half + pre * jnp.exp(-0.5 * pre * pre) * density_scale
    down = jnp.concatenate([down_own[0], down_pair[0]], 0)
    spread(dot(hidden, down, 1, 0), blocks, parts, held_refs, outs)


def spread(result, blocks, parts, held_refs, outs):
    block_rows = result.shape[0] // blocks
    for held_ref, ref in zip(held_refs, outs):
        ref[:, : held_ref.shape[1]] = held_ref[...]
    for number, (start, stop, slots) in enumerate(parts):
        for index, pair in enumerate(slots):
            for ref, block in zip(outs[2 * number : 2 * number + 2], pair):
                base = block * block_rows
                end = ref.shape[1]
                ref[index, end - (stop - start) : end] = result[
                    base + start : base + stop
                ].astype(jnp.bfloat16)


def backward_kernel(blocks, parts, held, *refs):
    grads = joined(refs[:blocks], refs[blocks : 2 * blocks])
    up_own, up_pair, down_own, down_pair, slope_ref = refs[2 * blocks : 2 * blocks + 5]
    held_refs = refs[2 * blocks + 5 : 2 * blocks + 5 + held]
    dpre_ref, *outs = refs[2 * blocks + 5 + held :]
    down = jnp.concatenate([down_own[0], down_pair[0]], 0)
    dpre = (dot(grads, down, 1, 1) * slope_ref[...]).astype(jnp.bfloat16)
    dpre_ref[...] = dpre
    up = jnp.concatenate([up_own[0], up_pair[0]], 0)
    spread(dot(dpre, up, 1, 0), blocks, parts, held_refs, outs)


def weight_kernel(blocks, *refs):
    rows = joined(refs[:blocks], refs[blocks : 2 * blocks])
    grads = joined(refs[2 * blocks : 3 * blocks], refs[3 * blocks : 4 * blocks])
    hidden_ref, dpre_ref, own_ref, pair_ref = refs[4 * blocks :]
    units = own_ref.shape[1]
    for index, (left_ref, right) in enumerate(((dpre_ref, rows), (hidden_ref, grads))):
        product = dot(left_ref[...], right, 0, 0)
        own_ref[index] = product[:units].astype(jnp.bfloat16)
        pair_ref[index] = product[units:].astype(jnp.bfloat16)


def total_kernel(local, *refs):
    own_refs = refs[:local]
    pair_refs = refs[local : 2 * local]
    out_refs = refs[2 * local :]
    for l in range(local):
        for index, ref in enumerate(out_refs):
            ref[l] = (
                own_refs[l][index].astype(jnp.float32) + pair_refs[l][index].astype(jnp.float32)
            ).astype(jnp.bfloat16)


def summed(refs):
    total = refs[0][0].astype(jnp.float32)
    for ref in refs[1:]:
        total = total + ref[0].astype(jnp.float32)
    return total.astype(jnp.bfloat16)


def finish_kernel(groups, *refs):
    outs = refs[sum(count for counts in groups for count in counts) :]
    cap = outs[0].shape[0] // len(groups)
    used = 0
    for l, counts in enumerate(groups):
        sums = []
        for count in counts:
            sums.append(summed(refs[used : used + count]))
            used += count
        low = jnp.concatenate(sums, 0)
        for index, out in enumerate(outs):
            out[l * cap : (l + 1) * cap] = low[index * cap : (index + 1) * cap]


def output_kernel(count, *refs):
    tok_ref, cot_ref, target_ref, weight_ref, alive_ref, out_ref, gating_ref = refs[-7:]
    results = jnp.concatenate(
        [summed(refs[:count])] + [ref[...] for ref in refs[count:-7]], 0
    )
    toks = tok_ref.shape[0]
    row = lax.broadcasted_iota(jnp.int32, (toks, toks), 0)
    same = row == lax.broadcasted_iota(jnp.int32, (toks, toks), 1)
    total = tok_ref[...].astype(jnp.float32)
    cot = cot_ref[...].astype(jnp.float32)
    for k in range(target_ref.shape[1]):
        picked = dot(one_hot(target_ref[:, k : k + 1], results.shape[0]), results, 1, 0)
        total = total + weight_ref[:, k : k + 1] * picked
        column = alive_ref[...] * jnp.sum(cot * picked, axis=1, keepdims=True)
        gating_ref[k : k + 1, :] = jnp.sum(jnp.where(same, column, 0.0), axis=0, keepdims=True)
    out_ref[...] = total.astype(jnp.bfloat16)


def input_kernel(count, *refs):
    tok_ref, cot_ref, target_ref, alive_ref, out_ref = refs[-5:]
    grads = jnp.concatenate([summed(refs[:count])] + [ref[...] for ref in refs[count:-5]], 0)
    hot = one_hot(target_ref[:, 0:1], grads.shape[0])
    for k in range(1, target_ref.shape[1]):
        hot = hot + one_hot(target_ref[:, k : k + 1], grads.shape[0])
    dnorm = alive_ref[...] * dot(hot, grads, 1, 0)
    normed, inv_scale = normalize(tok_ref[...])
    inner = jnp.mean(dnorm * normed, axis=1, keepdims=True)
    change = dnorm - jnp.mean(dnorm, axis=1, keepdims=True) - normed * inner
    out_ref[...] = (cot_ref[...].astype(jnp.float32) + inv_scale * change).astype(jnp.bfloat16)


def whole(array):
    rank = len(array.shape)
    return pl.BlockSpec(array.shape, lambda *_: (0,) * rank)


def part(array, index):
    rank = len(array.shape)
    return pl.BlockSpec((1,) + array.shape[1:], lambda *_: (index,) + (0,) * (rank - 1))


def slab(array, index, rows):
    return pl.BlockSpec((rows, array.shape[1]), lambda *_: (index, 0))


def spec_of(item):
    if not isinstance(item, tuple):
        return whole(item)
    return part(*item) if len(item) == 2 else slab(*item)


def run(kernel, inputs, outs):
    arrays = [item[0] if isinstance(item, tuple) else item for item in inputs]
    specs = [spec_of(item) for item in inputs]
    outs = [jax.ShapeDtypeStruct(shape, dtype) for shape, dtype in outs]
    return pl.pallas_call(
        kernel,
        out_shape=outs,
        grid=(1,),
        in_specs=specs,
        out_specs=[whole(out) for out in outs],
        compiler_params=pltpu.CompilerParams(vmem_limit_bytes=24 << 20),
    )(*arrays)


def body(
    tokens, cotangent, gate_weights, expert_ids, segments, keep_counts, expand_weight, reduce_weight
):
    toks, width = tokens.shape
    top = expert_ids.shape[1]
    groups = lax.axis_size("dp")
    planes = lax.axis_size("expert")
    local, units, _ = expand_weight.shape
    cap = top * toks // (planes * local)
    blocks = groups // 2
    bits = [1 << bit for bit in range(1, groups.bit_length() - 1)]
    block_rows = planes * cap
    low = jnp.bfloat16

    def swap(values, mask):
        return lax.ppermute(values, "dp", [(i, i ^ mask) for i in range(groups)])

    def cross(pieces):
        away = []
        for s, piece in enumerate(pieces, 1):
            away.append(lax.ppermute(piece, "expert", [(i, i ^ s) for i in range(planes)]))
        return away

    def order_of(name):
        shift = turns[name] % len(bits)
        return bits[shift:] + bits[:shift]

    def gather(name, own):
        held = {0: own}
        for bit in order_of(name):
            for block in sorted(held):
                held[block | bit] = swap(held[block], bit)
        return [held[2 * index] for index in range(blocks)]

    def part_of(name, start, stop):
        bit = order_of(name)[0] // 2
        slots = tuple((block | bit, block) for block in range(blocks) if not block & bit)
        return start, stop, slots

    def scatter(name, send, keep):
        order = order_of(name)
        bit = order[0]
        arrived = swap(send, bit)
        terms = {
            2 * slots[1]: [(keep, index), (arrived, index)]
            for index, slots in enumerate(part_of(name, 0, 0)[2])
        }
        for bit in order[1:]:
            leaving = [block for block in sorted(terms) if block & bit]
            sums = [
                run(add_kernel, terms[block], [((1,) + send.shape[1:], low)])[0]
                for block in leaving
            ]
            sums = sums[0] if len(sums) == 1 else jnp.concatenate(sums, 0)
            arrived = swap(sums, bit)
            for index, block in enumerate(leaving):
                terms[block ^ bit].append((arrived, index))
                del terms[block]
        return terms[0]

    me = lax.axis_index("expert").astype(jnp.int32).reshape(1)
    others = planes - 1
    near_parts = 1 if merge_near else 2
    feature_parts = 1 if merge_features else local
    grad_parts = local if split_grads else 1
    sources = [gate_weights.T, expert_ids.T, segments, keep_counts, tokens, cotangent]
    routed = pl.pallas_call(
        functools.partial(route_kernel, planes, local),
        out_shape=[jax.ShapeDtypeStruct((2 * local * cap // near_parts, width), low)] * near_parts
        + [jax.ShapeDtypeStruct((local * cap // feature_parts, width), low)]
        * (feature_parts * others)
        + [jax.ShapeDtypeStruct((local * cap // grad_parts, width), low)] * (grad_parts * others)
        + [
            jax.ShapeDtypeStruct((toks, top), jnp.int32),
            jax.ShapeDtypeStruct((toks, top), jnp.float32),
            jax.ShapeDtypeStruct((toks, 1), jnp.float32),
        ],
        in_specs=[pl.BlockSpec(memory_space=pltpu.SMEM)]
        + [pl.BlockSpec(memory_space=pltpu.HBM)] * len(sources),
        scratch_shapes=[pltpu.VMEM(source.shape, source.dtype) for source in sources]
        + [pltpu.SemaphoreType.DMA((len(sources),))],
        compiler_params=pltpu.CompilerParams(vmem_limit_bytes=24 << 20),
        name="route",
    )(me, *[pltpu.with_memory_space_constraint(source, pltpu.HBM) for source in sources])
    away = routed[near_parts:-3]
    target, weight, alive = routed[-3:]
    up_pair = swap(expand_weight, 1)
    down_pair = swap(reduce_weight, 1)

    far = others * cap
    if merge_near:
        near = gather("px", routed[0])
        near_features = [[(block, l, cap) for block in near] for l in range(local)]
        near_grads = [[(block, local + l, cap) for block in near] for l in range(local)]
    else:
        near_blocks = gather("px", routed[0]), gather("pg", routed[1])
        near_features, near_grads = [
            [[(block, l, cap) for block in held] for l in range(local)] for held in near_blocks
        ]

    def collect(name, pieces, split, merge):
        count = local if split else 1
        owns = []
        for index in range(count):
            arrived = cross(pieces[index * others : (index + 1) * others])
            owns += run(
                functools.partial(join_kernel, others, cap, merge),
                arrived,
                [((local * far if merge else far, width), low)]
                * (1 if merge else local // count),
            )
        if merge:
            held = gather(name, owns[0])
            return [[(block, l, far) for block in held] for l in range(local)]
        return [gather(f"{name}{l}", owns[l]) for l in range(local)]

    features = collect("x", away[: feature_parts * others], not merge_features, merge_features)
    features = [near_features[l] + features[l] for l in range(local)]
    grads = collect("g", away[feature_parts * others :], split_grads, merge_grads)
    grads = [near_grads[l] + grads[l] for l in range(local)]

    rows = blocks * block_rows
    flat = ((rows, 2 * units), low)
    wide = ((rows, 2 * units), jnp.float32)

    def outs_of(l, parts):
        sizes = [(l + 1) * cap] + [stop - start for start, stop, _ in parts[1:]]
        return [((blocks // 2, size, width), low) for size in sizes for _ in range(2)]

    hiddens, slopes, result_terms, held = [], [], [], []
    for l in range(local):
        parts = [part_of("py", 0, cap), part_of(f"y{l}", cap, block_rows)]
        hidden, slope, *sends = run(
            functools.partial(forward_kernel, blocks, parts, len(held)),
            features[l]
            + [(expand_weight, l), (up_pair, l), (reduce_weight, l), (down_pair, l)]
            + held,
            [flat, wide] + outs_of(l, parts),
        )
        hiddens.append(hidden)
        slopes.append(slope)
        held = sends[:2]
        result_terms.append([scatter(f"y{l}", sends[2], sends[3])])
    near_results = scatter("py", *held)
    dpres, input_terms, held = [], [], []
    for l in range(local):
        parts = [part_of("pd", 0, cap)]
        if split_inputs:
            half = cap + others * cap // 32 * 16
            named = [(f"d{l}0", cap, half), (f"d{l}1", half, block_rows)]
        else:
            named = [(f"d{l}", cap, block_rows)]
        parts += [part_of(*item) for item in named]
        dpre, *sends = run(
            functools.partial(backward_kernel, blocks, parts, len(held)),
            grads[l]
            + [(expand_weight, l), (up_pair, l), (reduce_weight, l), (down_pair, l), slopes[l]]
            + held,
            [flat] + outs_of(l, parts),
        )
        dpres.append(dpre)
        held = sends[:2]
        input_terms.append(
            [
                scatter(item[0], *sends[2 * index + 2 : 2 * index + 4])
                for index, item in enumerate(named)
            ]
        )
    near_inputs = scatter("pd", *held)
    owns, pairs = [], []
    for l in range(local):
        own, pair = run(
            functools.partial(weight_kernel, blocks),
            features[l] + grads[l] + [hiddens[l], dpres[l]],
            [((2, units, width), low)] * 2,
        )
        owns.append(own)
        pairs.append(swap(pair, 1))
    expand_grad, reduce_grad = run(
        functools.partial(total_kernel, local), owns + pairs, [(expand_weight.shape, low)] * 2
    )

    def finish(terms_list):
        groups = [[len(terms) for terms in parts] for parts in terms_list]
        outs = run(
            functools.partial(finish_kernel, groups),
            [item for parts in terms_list for terms in parts for item in terms],
            [((len(terms_list) * cap, width), low)] * others,
        )
        return cross(outs)

    if split_results:
        returned = [finish([result_terms[l]]) for l in range(local)]
        returned = [returned[l][s] for s in range(others) for l in range(local)]
    else:
        returned = finish(result_terms)
    output, gating_grad = run(
        functools.partial(output_kernel, len(near_results)),
        near_results + returned + [tokens, cotangent, target, weight, alive],
        [(tokens.shape, low), ((top, toks), jnp.float32)],
    )
    back = [finish([input_terms[l]]) for l in range(local)]
    (tokens_grad,) = run(
        functools.partial(input_kernel, len(near_inputs)),
        near_inputs
        + [back[l][s] for s in range(others) for l in range(local)]
        + [tokens, cotangent, target, alive],
        [(tokens.shape, low)],
    )
    return (output, tokens_grad, gating_grad.T, expand_grad, reduce_grad)


def solution(mesh):
    rows = P(("dp", "expert"), None)
    weights = P("expert", "dp", None)

    return jax.shard_map(
        body,
        mesh=mesh,
        in_specs=(rows,) * 6 + (weights,) * 2,
        out_specs=(rows,) * 3 + (weights,) * 2,
        check_vma=False,
    )
```

profile of v0, /device:TPU:0, one launch (start us, length us, event | category | flops | bytes accessed | tf_op | source)
XLA Modules:
  0.0 180.1 jit_solution(6164304918887568573)
XLA Ops:
  1.3 2.1 %route.1 = (bf16[64,1280]{1,0:T(8,128)(2,1)S(1)}, bf16[64,1280]{1,0:T(8,128)(2,1)S(1)}, bf16[32,1280]{1,0:T(8,128)(2,1)S(1)}, bf16[32,1280]{1,0:T(8,128)(2,1)S(1...) custom-call(s32[1]{0:T(128)} %bitcast.me_ref, ...), custom_call_target="tpu_custom_call" | custom-call | tf_op jit(solution)/shard_map/route/pallas_call | solution.py:379
  3.4 3.1 %collective-permute-start.3 = (bf16[32,1280]{1,0:T(8,128)(2,1)S(1)}, bf16[32,1280]{1,0:T(8,128)(2,1)S(1)}, u32[]{:S(2)}, u32[]{:S(2)}) collective-permute-start(bf16[32,1280]{1,0:T(8,128)(2,1)S(1)} %get-tuple-element.61), channel_id=1, source_target_pairs={{0,1},{1,0},{2,3},{3,2},{4,5},{5,4},{6,7},{7,6},{8,9},{9,8},{10,11... | collective-permute-start | bytes 245768 | tf_op jit(solution)/shard_map/ppermute | solution.py:333
  6.4 2.6 %collective-permute-start.4 = (bf16[32,1280]{1,0:T(8,128)(2,1)S(1)}, bf16[32,1280]{1,0:T(8,128)(2,1)S(1)}, u32[]{:S(2)}, u32[]{:S(2)}) collective-permute-start(bf16[32,1280]{1,0:T(8,128)(2,1)S(1)} %get-tuple-element.62), channel_id=1, source_target_pairs={{0,2},{1,3},{2,0},{3,1},{4,6},{5,7},{6,4},{7,5},{8,10},{9,11},{10,... | collective-permute-start | bytes 245768 | tf_op jit(solution)/shard_map/ppermute | solution.py:333
  9.1 1.8 collective-permute-start.11
  10.9 5.0 %collective-permute-done.4.refs_1_ = bf16[32,1280]{1,0:T(8,128)(2,1)S(1)} collective-permute-done((bf16[32,1280]{1,0:T(8,128)(2,1)S(1)}, bf16[32,1280]{1,0:T(8,128)(2,1)S(1)}, u32[]{:S(2)}, u32[]{:S(2)}) %collective-permute-start.4) | collective-permute-done | bytes 81952 | tf_op jit(solution)/shard_map/ppermute | solution.py:333
  15.9 1.5 collective-permute-start
  18.3 1.6 collective-permute-start.13
  19.9 5.0 %collective-permute-done.12.refs_1_ = bf16[32,1280]{1,0:T(8,128)(2,1)S(1)} collective-permute-done((bf16[32,1280]{1,0:T(8,128)(2,1)S(1)}, bf16[32,1280]{1,0:T(8,128)(2,1)S(1)}, u32[]{:S(2)}, u32[]{:S(2)}) %collective-permute-start.12) | collective-permute-done | bytes 81952 | tf_op jit(solution)/shard_map/ppermute | solution.py:333
  24.9 1.5 collective-permute-start.1
  27.7 2.6 %collective-permute-done.1.refs_2_ = bf16[64,1280]{1,0:T(8,128)(2,1)S(1)} collective-permute-done((bf16[64,1280]{1,0:T(8,128)(2,1)S(1)}, bf16[64,1280]{1,0:T(8,128)(2,1)S(1)}, u32[]{:S(2)}, u32[]{:S(2)}) %collective-permute-start.1) | collective-permute-done | bytes 163872 | tf_op jit(solution)/shard_map/ppermute | solution.py:328
  30.3 1.5 collective-permute-done.26.refs_1_.refs_9_
  32.6 2.4 %collective-permute-start.31 = (bf16[64,1280]{1,0:T(8,128)(2,1)S(1)}, bf16[64,1280]{1,0:T(8,128)(2,1)S(1)}, u32[]{:S(2)}, u32[]{:S(2)}) collective-permute-start(bf16[64,1280]{1,0:T(8,128)(2,1)S(1)} %get-tuple-element.85), channel_id=1, source_target_pairs={{0,3},{1,2},{2,1},{3,0},{4,7},{5,6},{6,5},{7,4},{8,11},{9,10},{10,... | collective-permute-start | bytes 491528 | tf_op jit(solution)/shard_map/ppermute | solution.py:333
  35.0 2.3 %collective-permute-done.29.refs_0_ = bf16[64,1280]{1,0:T(8,128)(2,1)S(1)} collective-permute-done((bf16[64,1280]{1,0:T(8,128)(2,1)S(1)}, bf16[64,1280]{1,0:T(8,128)(2,1)S(1)}, u32[]{:S(2)}, u32[]{:S(2)}) %collective-permute-start.29) | collective-permute-done | bytes 163872 | tf_op jit(solution)/shard_map/ppermute | solution.py:333
  37.4 1.5 collective-permute-start.6
  38.9 3.5 %collective-permute-done.30.refs_1_ = bf16[64,1280]{1,0:T(8,128)(2,1)S(1)} collective-permute-done((bf16[64,1280]{1,0:T(8,128)(2,1)S(1)}, bf16[64,1280]{1,0:T(8,128)(2,1)S(1)}, u32[]{:S(2)}, u32[]{:S(2)}) %collective-permute-start.30) | collective-permute-done | bytes 163872 | tf_op jit(solution)/shard_map/ppermute | solution.py:333
  44.5 10.2 %collective-permute-done.2.refs_3_ = bf16[64,1280]{1,0:T(8,128)(2,1)S(1)} collective-permute-done((bf16[64,1280]{1,0:T(8,128)(2,1)S(1)}, bf16[64,1280]{1,0:T(8,128)(2,1)S(1)}, u32[]{:S(2)}, u32[]{:S(2)}) %collective-permute-start.2) | collective-permute-done | bytes 163872 | tf_op jit(solution)/shard_map/ppermute | solution.py:328
  55.6 1.5 collective-permute-start.15
  57.6 5.1 %collective-permute-done.14.refs_5_ = bf16[96,1280]{1,0:T(8,128)(2,1)S(1)} collective-permute-done((bf16[96,1280]{1,0:T(8,128)(2,1)S(1)}, bf16[96,1280]{1,0:T(8,128)(2,1)S(1)}, u32[]{:S(2)}, u32[]{:S(2)}) %collective-permute-start.14) | collective-permute-done | bytes 245792 | tf_op jit(solution)/shard_map/ppermute | solution.py:328
  65.6 4.1 %collective-permute-done.33.refs_6_.refs_14_ = bf16[96,1280]{1,0:T(8,128)(2,1)S(1)} collective-permute-done((bf16[96,1280]{1,0:T(8,128)(2,1)S(1)}, bf16[96,1280]{1,0:T(8,128)(2,1)S(1)}, u32[]{:S(2)}, u32[]{:S(2)}) %collective-permute-start.33) | collective-permute-done | bytes 245792 | tf_op jit(solution)/shard_map/ppermute | solution.py:328
  69.7 1.5 collective-permute-start.16
  72.3 3.6 %collective-permute-done.8.refs_7_ = bf16[96,1280]{1,0:T(8,128)(2,1)S(1)} collective-permute-done((bf16[96,1280]{1,0:T(8,128)(2,1)S(1)}, bf16[96,1280]{1,0:T(8,128)(2,1)S(1)}, u32[]{:S(2)}, u32[]{:S(2)}) %collective-permute-start.8) | collective-permute-done | bytes 245792 | tf_op jit(solution)/shard_map/ppermute | solution.py:328
  76.3 2.5 %collective-permute-start.37 = (bf16[96,1280]{1,0:T(8,128)(2,1)S(1)}, bf16[96,1280]{1,0:T(8,128)(2,1)S(1)}, u32[]{:S(2)}, u32[]{:S(2)}) collective-permute-start(bf16[96,1280]{1,0:T(8,128)(2,1)S(1)} %collective-permute-done.35.refs_5_.refs_13_), channel_id=1, source_target_pairs={{0,16},{4,20},{8,24},{12,28},{16,0},{20,4},{24,8},{28,12},{1,17},{... | collective-permute-start | bytes 737288 | tf_op jit(solution)/shard_map/ppermute | solution.py:328
  82.2 3.7 %shard_map.121 = (bf16[512,640]{1,0:T(8,128)(2,1)S(1)}, f32[512,640]{1,0:T(8,128)S(1)}, bf16[2,32,1280]{2,1,0:T(8,128)(2,1)S(1)}, bf16[2,32,1280]{2,1,0:T(8,128)...) custom-call(bf16[64,1280]{1,0:T(8,128)(2,1)S(1)} %get-tuple-element.60.refs_0_, ...), custom_call_target="tpu_custom_call" | custom-call | tf_op jit(solution)/shard_map/pallas_call | solution.py:303
  85.9 3.6 %shard_map.122 = (bf16[512,640]{1,0:T(8,128)(2,1)S(1)}, f32[512,640]{1,0:T(8,128)S(1)}, bf16[2,64,1280]{2,1,0:T(8,128)(2,1)S(1)}, bf16[2,64,1280]{2,1,0:T(8,128)...) custom-call(bf16[64,1280]{1,0:T(8,128)(2,1)S(1)} %get-tuple-element.60.refs_0_, ...), custom_call_target="tpu_custom_call" | custom-call | tf_op jit(solution)/shard_map/pallas_call | solution.py:303
  89.6 3.5 %shard_map.129 = (bf16[512,640]{1,0:T(8,128)(2,1)S(1)}, bf16[2,32,1280]{2,1,0:T(8,128)(2,1)S(1)}, bf16[2,32,1280]{2,1,0:T(8,128)(2,1)S(1)}, bf16[2,96,1280]{2,1,0:T(8,128)(2,1)S(1)}, bf16[2,96,1280]{2,1,0:T(8,128)(2,1)S(1)}) custom-call(bf16[64,1280]{1,0:T(8,128)(2,1)S(1)} %get-tuple-element.82.refs_0_.refs_8_, ...), custom_call_target="tpu_custom_call" | custom-call | tf_op jit(solution)/shard_map/pallas_call | solution.py:303
  93.1 3.5 %shard_map.130 = (bf16[512,640]{1,0:T(8,128)(2,1)S(1)}, bf16[2,64,1280]{2,1,0:T(8,128)(2,1)S(1)}, bf16[2,64,1280]{2,1,0:T(8,128)(2,1)S(1)}, bf16[2,96,1280]{2,1,0:T(8,128)(2,1)S(1)}, bf16[2,96,1280]{2,1,0:T(8,128)(2,1)S(1)}) custom-call(bf16[64,1280]{1,0:T(8,128)(2,1)S(1)} %get-tuple-element.82.refs_0_.refs_8_, ...), custom_call_target="tpu_custom_call" | custom-call | tf_op jit(solution)/shard_map/pallas_call | solution.py:303
  98.1 2.1 %shard_map.137 = (bf16[2,320,1280]{2,1,0:T(8,128)(2,1)S(1)}, bf16[2,320,1280]{2,1,0:T(8,128)(2,1)S(1)}) custom-call(bf16[64,1280]{1,0:T(8,128)(2,1)S(1)} %get-tuple-element.60.refs_0_, bf16[64,1280]{1,0:T(8,128)(2,1)S(1)} %collective-permute-done.refs_1_, bf16[64,1280]{1,0:T(8,128)(2,1)S(1)} %collective-permute-done.1.refs_2_, ...), custom_call_target="tpu_custom_call" | custom-call | tf_op jit(solution)/shard_map/pallas_call | solution.py:303
  100.3 1.9 %shard_map.138 = (bf16[2,320,1280]{2,1,0:T(8,128)(2,1)S(1)}, bf16[2,320,1280]{2,1,0:T(8,128)(2,1)S(1)}) custom-call(bf16[64,1280]{1,0:T(8,128)(2,1)S(1)} %get-tuple-element.60.refs_0_, bf16[64,1280]{1,0:T(8,128)(2,1)S(1)} %collective-permute-done.refs_1_, bf16[64,1280]{1,0:T(8,128)(2,1)S(1)} %collective-permute-done.1.refs_2_, ...), custom_call_target="tpu_custom_call" | custom-call | tf_op jit(solution)/shard_map/pallas_call | solution.py:303
  104.9 2.0 %collective-permute-start.43 = (bf16[2,96,1280]{2,1,0:T(8,128)(2,1)S(1)}, bf16[2,96,1280]{2,1,0:T(8,128)(2,1)S(1)}, u32[]{:S(2)}, u32[]{:S(2)}) collective-permute-start(bf16[2,96,1280]{2,1,0:T(8,128)(2,1)S(1)} %get-tuple-element.98), channel_id=1, source_target_pairs={{0,16},{4,20},{8,24},{12,28},{16,0},{20,4},{24,8},{28,12},{1,17},{... | collective-permute-start | bytes 1474568 | tf_op jit(solution)/shard_map/ppermute | solution.py:328
  106.8 12.6 %collective-permute-done.18.refs_2_ = bf16[1,64,1280]{2,1,0:T(8,128)(2,1)S(1)} collective-permute-done((bf16[1,64,1280]{2,1,0:T(8,128)(2,1)S(1)}, bf16[1,64,1280]{2,1,0:T(8,128)(2,1)S(1)}, u32[]{:S(2)}, u32[]{:S(2)}) %collective-permute-start.18) | collective-permute-done | bytes 163872 | tf_op jit(solution)/shard_map/ppermute | solution.py:328
  120.1 2.0 %collective-permute-start.21 = (bf16[2,96,1280]{2,1,0:T(8,128)(2,1)S(1)}, bf16[2,96,1280]{2,1,0:T(8,128)(2,1)S(1)}, u32[]{:S(2)}, u32[]{:S(2)}) collective-permute-start(bf16[2,96,1280]{2,1,0:T(8,128)(2,1)S(1)} %get-tuple-element.74), channel_id=1, source_target_pairs={{0,16},{4,20},{8,24},{12,28},{16,0},{20,4},{24,8},{28,12},{1,17},{... | collective-permute-start | bytes 1474568 | tf_op jit(solution)/shard_map/ppermute | solution.py:328
  122.3 9.5 %collective-permute-done.19.refs_1_ = bf16[2,96,1280]{2,1,0:T(8,128)(2,1)S(1)} collective-permute-done((bf16[2,96,1280]{2,1,0:T(8,128)(2,1)S(1)}, bf16[2,96,1280]{2,1,0:T(8,128)(2,1)S(1)}, u32[]{:S(2)}, u32[]{:S(2)}) %collective-permute-start.19) | collective-permute-done | bytes 491552 | tf_op jit(solution)/shard_map/ppermute | solution.py:328
  132.5 1.7 collective-permute-done.21.refs_1_.refs_4_
  134.2 2.0 %collective-permute-start.20 = (bf16[1,96,1280]{2,1,0:T(8,128)(2,1)S(1)}, bf16[1,96,1280]{2,1,0:T(8,128)(2,1)S(1)}, u32[]{:S(2)}, u32[]{:S(2)}) collective-permute-start(bf16[1,96,1280]{2,1,0:T(8,128)(2,1)S(1)} %shard_map.124), channel_id=1, source_target_pairs={{0,16},{4,20},{8,24},{12,28},{16,0},{20,4},{24,8},{28,12},{1,17},{... | collective-permute-start | bytes 737288 | tf_op jit(solution)/shard_map/ppermute | solution.py:328
  136.3 3.2 %collective-permute-done.41.refs_2_ = bf16[1,96,1280]{2,1,0:T(8,128)(2,1)S(1)} collective-permute-done((bf16[1,96,1280]{2,1,0:T(8,128)(2,1)S(1)}, bf16[1,96,1280]{2,1,0:T(8,128)(2,1)S(1)}, u32[]{:S(2)}, u32[]{:S(2)}) %collective-permute-start.41) | collective-permute-done | bytes 245792 | tf_op jit(solution)/shard_map/ppermute | solution.py:328
  140.9 2.1 %collective-permute-start.39 = (bf16[1,64,1280]{2,1,0:T(8,128)(2,1)S(1)}, bf16[1,64,1280]{2,1,0:T(8,128)(2,1)S(1)}, u32[]{:S(2)}, u32[]{:S(2)}) collective-permute-start(bf16[1,64,1280]{2,1,0:T(8,128)(2,1)S(1)} %shard_map.131), channel_id=1, source_target_pairs={{0,16},{4,20},{8,24},{12,28},{16,0},{20,4},{24,8},{28,12},{1,17},{... | collective-permute-start | bytes 491528 | tf_op jit(solution)/shard_map/ppermute | solution.py:328
  143.2 3.3 %collective-permute-done.39.refs_2_ = bf16[1,64,1280]{2,1,0:T(8,128)(2,1)S(1)} collective-permute-done((bf16[1,64,1280]{2,1,0:T(8,128)(2,1)S(1)}, bf16[1,64,1280]{2,1,0:T(8,128)(2,1)S(1)}, u32[]{:S(2)}, u32[]{:S(2)}) %collective-permute-start.39) | collective-permute-done | bytes 163872 | tf_op jit(solution)/shard_map/ppermute | solution.py:328
  146.5 2.0 %collective-permute-start.45 = (bf16[32,1280]{1,0:T(8,128)(2,1)S(1)}, bf16[32,1280]{1,0:T(8,128)(2,1)S(1)}, u32[]{:S(2)}, u32[]{:S(2)}) collective-permute-start(bf16[32,1280]{1,0:T(8,128)(2,1)S(1)} %get-tuple-element.99), channel_id=1, source_target_pairs={{0,1},{1,0},{2,3},{3,2},{4,5},{5,4},{6,7},{7,6},{8,9},{9,8},{10,11... | collective-permute-start | bytes 245768 | tf_op jit(solution)/shard_map/ppermute | solution.py:333
  148.5 1.7 collective-permute-start.46
  151.5 1.9 %collective-permute-start.47 = (bf16[32,1280]{1,0:T(8,128)(2,1)S(1)}, bf16[32,1280]{1,0:T(8,128)(2,1)S(1)}, u32[]{:S(2)}, u32[]{:S(2)}) collective-permute-start(bf16[32,1280]{1,0:T(8,128)(2,1)S(1)} %get-tuple-element.101), channel_id=1, source_target_pairs={{0,2},{1,3},{2,0},{3,1},{4,6},{5,7},{6,4},{7,5},{8,10},{9,11},{10,... | collective-permute-start | bytes 245768 | tf_op jit(solution)/shard_map/ppermute | solution.py:333
  153.4 2.5 %collective-permute-start.48 = (bf16[32,1280]{1,0:T(8,128)(2,1)S(1)}, bf16[32,1280]{1,0:T(8,128)(2,1)S(1)}, u32[]{:S(2)}, u32[]{:S(2)}) collective-permute-start(bf16[32,1280]{1,0:T(8,128)(2,1)S(1)} %get-tuple-element.102), channel_id=1, source_target_pairs={{0,3},{1,2},{2,1},{3,0},{4,7},{5,6},{6,5},{7,4},{8,11},{9,10},{10,... | collective-permute-start | bytes 245768 | tf_op jit(solution)/shard_map/ppermute | solution.py:333
  155.9 2.9 %collective-permute-done.46.refs_5_ = bf16[32,1280]{1,0:T(8,128)(2,1)S(1)} collective-permute-done((bf16[32,1280]{1,0:T(8,128)(2,1)S(1)}, bf16[32,1280]{1,0:T(8,128)(2,1)S(1)}, u32[]{:S(2)}, u32[]{:S(2)}) %collective-permute-start.46) | collective-permute-done | bytes 81952 | tf_op jit(solution)/shard_map/ppermute | solution.py:333
  158.8 2.0 %collective-permute-start.49 = (bf16[32,1280]{1,0:T(8,128)(2,1)S(1)}, bf16[32,1280]{1,0:T(8,128)(2,1)S(1)}, u32[]{:S(2)}, u32[]{:S(2)}) collective-permute-start(bf16[32,1280]{1,0:T(8,128)(2,1)S(1)} %get-tuple-element.103), channel_id=1, source_target_pairs={{0,3},{1,2},{2,1},{3,0},{4,7},{5,6},{6,5},{7,4},{8,11},{9,10},{10,... | collective-permute-start | bytes 245768 | tf_op jit(solution)/shard_map/ppermute | solution.py:333
  161.5 2.9 %collective-permute-start.24 = (bf16[64,1280]{1,0:T(8,128)(2,1)S(1)}, bf16[64,1280]{1,0:T(8,128)(2,1)S(1)}, u32[]{:S(2)}, u32[]{:S(2)}) collective-permute-start(bf16[64,1280]{1,0:T(8,128)(2,1)S(1)} %get-tuple-element.76), channel_id=1, source_target_pairs={{0,2},{1,3},{2,0},{3,1},{4,6},{5,7},{6,4},{7,5},{8,10},{9,11},{10,... | collective-permute-start | bytes 491528 | tf_op jit(solution)/shard_map/ppermute | solution.py:333
  164.4 1.7 collective-permute-done.49.refs_8_
  166.1 2.0 %collective-permute-start.25 = (bf16[64,1280]{1,0:T(8,128)(2,1)S(1)}, bf16[64,1280]{1,0:T(8,128)(2,1)S(1)}, u32[]{:S(2)}, u32[]{:S(2)}) collective-permute-start(bf16[64,1280]{1,0:T(8,128)(2,1)S(1)} %get-tuple-element.77), channel_id=1, source_target_pairs={{0,3},{1,2},{2,1},{3,0},{4,7},{5,6},{6,5},{7,4},{8,11},{9,10},{10,... | collective-permute-start | bytes 491528 | tf_op jit(solution)/shard_map/ppermute | solution.py:333
  169.9 6.3 %collective-permute-done.24.refs_4_ = bf16[64,1280]{1,0:T(8,128)(2,1)S(1)} collective-permute-done((bf16[64,1280]{1,0:T(8,128)(2,1)S(1)}, bf16[64,1280]{1,0:T(8,128)(2,1)S(1)}, u32[]{:S(2)}, u32[]{:S(2)}) %collective-permute-start.24) | collective-permute-done | bytes 163872 | tf_op jit(solution)/shard_map/ppermute | solution.py:333
  177.7 2.4 %shard_map.139 = (bf16[2,320,1280]{2,1,0:T(8,128)(2,1)}, bf16[2,320,1280]{2,1,0:T(8,128)(2,1)}) custom-call(bf16[2,320,1280]{2,1,0:T(8,128)(2,1)S(1)} %get-tuple-element.107.refs_0_, bf16[2,320,1280]{2,1,0:T(8,128)(2,1)S(1)} %get-tuple-element.110.refs_1_, bf16[2,320,1280]{2,1,0:T(8,128)(2,1)S(1)} %collective-permute-done.50.refs_2_, ...), custom_call_target="tpu_custom_call" | custom-call | tf_op jit(solution)/shard_map/pallas_call | solution.py:303
  (88 shorter events, 27.8 us)
Async XLA Ops:
  0.6 78.1 %collective-permute-start.9 = (bf16[2,320,1280]{2,1,0:T(8,128)(2,1)}, bf16[2,320,1280]{2,1,0:T(8,128)(2,1)S(1)}, u32[]{:S(2)}, u32[]{:S(2)}) collective-permute-start(bf16[2,320,1280]{2,1,0:T(8,128)(2,1)} %refs_8_.7), channel_id=1, source_target_pairs={{0,4},{4,0},{8,12},{12,8},{16,20},{20,16},{24,28},{28,24},{1,5},{5... | collective-permute-start | bytes 4915208 | tf_op jit(solution)/shard_map/ppermute | solution.py:328
  1.2 78.9 %collective-permute-start.10 = (bf16[2,320,1280]{2,1,0:T(8,128)(2,1)}, bf16[2,320,1280]{2,1,0:T(8,128)(2,1)}, u32[]{:S(2)}, u32[]{:S(2)}) collective-permute-start(bf16[2,320,1280]{2,1,0:T(8,128)(2,1)} %refs_10_.8), channel_id=1, source_target_pairs={{0,4},{4,0},{8,12},{12,8},{16,20},{20,16},{24,28},{28,24},{1,5},{5... | collective-permute-start | bytes 4915208 | tf_op jit(solution)/shard_map/ppermute | solution.py:328
  3.4 5.7 %collective-permute-start.3 = (bf16[32,1280]{1,0:T(8,128)(2,1)S(1)}, bf16[32,1280]{1,0:T(8,128)(2,1)S(1)}, u32[]{:S(2)}, u32[]{:S(2)}) collective-permute-start(bf16[32,1280]{1,0:T(8,128)(2,1)S(1)} %get-tuple-element.61), channel_id=1, source_target_pairs={{0,1},{1,0},{2,3},{3,2},{4,5},{5,4},{6,7},{7,6},{8,9},{9,8},{10,11... | collective-permute-start | bytes 245768 | tf_op jit(solution)/shard_map/ppermute | solution.py:333
  6.4 9.4 %collective-permute-start.4 = (bf16[32,1280]{1,0:T(8,128)(2,1)S(1)}, bf16[32,1280]{1,0:T(8,128)(2,1)S(1)}, u32[]{:S(2)}, u32[]{:S(2)}) collective-permute-start(bf16[32,1280]{1,0:T(8,128)(2,1)S(1)} %get-tuple-element.62), channel_id=1, source_target_pairs={{0,2},{1,3},{2,0},{3,1},{4,6},{5,7},{6,4},{7,5},{8,10},{9,11},{10,... | collective-permute-start | bytes 245768 | tf_op jit(solution)/shard_map/ppermute | solution.py:333
  9.0 8.3 %collective-permute-start.5 = (bf16[32,1280]{1,0:T(8,128)(2,1)S(1)}, bf16[32,1280]{1,0:T(8,128)(2,1)S(1)}, u32[]{:S(2)}, u32[]{:S(2)}) collective-permute-start(bf16[32,1280]{1,0:T(8,128)(2,1)S(1)} %get-tuple-element.63), channel_id=1, source_target_pairs={{0,3},{1,2},{2,1},{3,0},{4,7},{5,6},{6,5},{7,4},{8,11},{9,10},{10,... | collective-permute-start | bytes 245768 | tf_op jit(solution)/shard_map/ppermute | solution.py:333
  9.1 9.2 %collective-permute-start.11 = (bf16[32,1280]{1,0:T(8,128)(2,1)S(1)}, bf16[32,1280]{1,0:T(8,128)(2,1)S(1)}, u32[]{:S(2)}, u32[]{:S(2)}) collective-permute-start(bf16[32,1280]{1,0:T(8,128)(2,1)S(1)} %get-tuple-element.64), channel_id=1, source_target_pairs={{0,1},{1,0},{2,3},{3,2},{4,5},{5,4},{6,7},{7,6},{8,9},{9,8},{10,11... | collective-permute-start | bytes 245768 | tf_op jit(solution)/shard_map/ppermute | solution.py:333
  15.9 10.7 %collective-permute-start = (bf16[64,1280]{1,0:T(8,128)(2,1)S(1)}, bf16[64,1280]{1,0:T(8,128)(2,1)S(1)}, u32[]{:S(2)}, u32[]{:S(2)}) collective-permute-start(bf16[64,1280]{1,0:T(8,128)(2,1)S(1)} %get-tuple-element.60.refs_0_), channel_id=1, source_target_pairs={{0,8},{4,12},{8,0},{12,4},{16,24},{20,28},{24,16},{28,20},{1,9},{5... | collective-permute-start | bytes 491528 | tf_op jit(solution)/shard_map/ppermute | solution.py:328
  17.4 7.5 %collective-permute-start.12 = (bf16[32,1280]{1,0:T(8,128)(2,1)S(1)}, bf16[32,1280]{1,0:T(8,128)(2,1)S(1)}, u32[]{:S(2)}, u32[]{:S(2)}) collective-permute-start(bf16[32,1280]{1,0:T(8,128)(2,1)S(1)} %get-tuple-element.65), channel_id=1, source_target_pairs={{0,2},{1,3},{2,0},{3,1},{4,6},{5,7},{6,4},{7,5},{8,10},{9,11},{10,... | collective-permute-start | bytes 245768 | tf_op jit(solution)/shard_map/ppermute | solution.py:333
  18.3 8.1 %collective-permute-start.13 = (bf16[32,1280]{1,0:T(8,128)(2,1)S(1)}, bf16[32,1280]{1,0:T(8,128)(2,1)S(1)}, u32[]{:S(2)}, u32[]{:S(2)}) collective-permute-start(bf16[32,1280]{1,0:T(8,128)(2,1)S(1)} %get-tuple-element.66), channel_id=1, source_target_pairs={{0,3},{1,2},{2,1},{3,0},{4,7},{5,6},{6,5},{7,4},{8,11},{9,10},{10,... | collective-permute-start | bytes 245768 | tf_op jit(solution)/shard_map/ppermute | solution.py:333
  26.5 6.0 %collective-permute-start.27 = (bf16[64,1280]{1,0:T(8,128)(2,1)S(1)}, bf16[64,1280]{1,0:T(8,128)(2,1)S(1)}, u32[]{:S(2)}, u32[]{:S(2)}) collective-permute-start(bf16[64,1280]{1,0:T(8,128)(2,1)S(1)} %get-tuple-element.82.refs_0_.refs_8_), channel_id=1, source_target_pairs={{0,16},{4,20},{8,24},{12,28},{16,0},{20,4},{24,8},{28,12},{1,17},{... | collective-permute-start | bytes 491528 | tf_op jit(solution)/shard_map/ppermute | solution.py:328
  30.3 7.1 %collective-permute-start.29 = (bf16[64,1280]{1,0:T(8,128)(2,1)S(1)}, bf16[64,1280]{1,0:T(8,128)(2,1)S(1)}, u32[]{:S(2)}, u32[]{:S(2)}) collective-permute-start(bf16[64,1280]{1,0:T(8,128)(2,1)S(1)} %get-tuple-element.83), channel_id=1, source_target_pairs={{0,1},{1,0},{2,3},{3,2},{4,5},{5,4},{6,7},{7,6},{8,9},{9,8},{10,11... | collective-permute-start | bytes 491528 | tf_op jit(solution)/shard_map/ppermute | solution.py:333
  31.7 10.6 %collective-permute-start.30 = (bf16[64,1280]{1,0:T(8,128)(2,1)S(1)}, bf16[64,1280]{1,0:T(8,128)(2,1)S(1)}, u32[]{:S(2)}, u32[]{:S(2)}) collective-permute-start(bf16[64,1280]{1,0:T(8,128)(2,1)S(1)} %get-tuple-element.84), channel_id=1, source_target_pairs={{0,2},{1,3},{2,0},{3,1},{4,6},{5,7},{6,4},{7,5},{8,10},{9,11},{10,... | collective-permute-start | bytes 491528 | tf_op jit(solution)/shard_map/ppermute | solution.py:333
  32.6 11.0 %collective-permute-start.31 = (bf16[64,1280]{1,0:T(8,128)(2,1)S(1)}, bf16[64,1280]{1,0:T(8,128)(2,1)S(1)}, u32[]{:S(2)}, u32[]{:S(2)}) collective-permute-start(bf16[64,1280]{1,0:T(8,128)(2,1)S(1)} %get-tuple-element.85), channel_id=1, source_target_pairs={{0,3},{1,2},{2,1},{3,0},{4,7},{5,6},{6,5},{7,4},{8,11},{9,10},{10,... | collective-permute-start | bytes 491528 | tf_op jit(solution)/shard_map/ppermute | solution.py:333
  37.4 18.2 %collective-permute-start.6 = (bf16[96,1280]{1,0:T(8,128)(2,1)S(1)}, bf16[96,1280]{1,0:T(8,128)(2,1)S(1)}, u32[]{:S(2)}, u32[]{:S(2)}) collective-permute-start(bf16[96,1280]{1,0:T(8,128)(2,1)S(1)} %shard_map.119.refs_4_), channel_id=1, source_target_pairs={{0,8},{4,12},{8,0},{12,4},{16,24},{20,28},{24,16},{28,20},{1,9},{5... | collective-permute-start | bytes 737288 | tf_op jit(solution)/shard_map/ppermute | solution.py:328
  42.4 14.7 %collective-permute-start.7 = (bf16[96,1280]{1,0:T(8,128)(2,1)S(1)}, bf16[96,1280]{1,0:T(8,128)(2,1)S(1)}, u32[]{:S(2)}, u32[]{:S(2)}) collective-permute-start(bf16[96,1280]{1,0:T(8,128)(2,1)S(1)} %shard_map.119.refs_4_), channel_id=1, source_target_pairs={{0,16},{4,20},{8,24},{12,28},{16,0},{20,4},{24,8},{28,12},{1,17},{... | collective-permute-start | bytes 737288 | tf_op jit(solution)/shard_map/ppermute | solution.py:328
  43.6 11.1 %collective-permute-start.2 = (bf16[64,1280]{1,0:T(8,128)(2,1)S(1)}, bf16[64,1280]{1,0:T(8,128)(2,1)S(1)}, u32[]{:S(2)}, u32[]{:S(2)}) collective-permute-start(bf16[64,1280]{1,0:T(8,128)(2,1)S(1)} %collective-permute-done.refs_1_), channel_id=1, source_target_pairs={{0,16},{4,20},{8,24},{12,28},{16,0},{20,4},{24,8},{28,12},{1,17},{... | collective-permute-start | bytes 491528 | tf_op jit(solution)/shard_map/ppermute | solution.py:328
  54.7 8.0 %collective-permute-start.14 = (bf16[96,1280]{1,0:T(8,128)(2,1)S(1)}, bf16[96,1280]{1,0:T(8,128)(2,1)S(1)}, u32[]{:S(2)}, u32[]{:S(2)}) collective-permute-start(bf16[96,1280]{1,0:T(8,128)(2,1)S(1)} %shard_map.120.refs_4_), channel_id=1, source_target_pairs={{0,8},{4,12},{8,0},{12,4},{16,24},{20,28},{24,16},{28,20},{1,9},{5... | collective-permute-start | bytes 737288 | tf_op jit(solution)/shard_map/ppermute | solution.py:328
  55.6 8.8 %collective-permute-start.15 = (bf16[96,1280]{1,0:T(8,128)(2,1)S(1)}, bf16[96,1280]{1,0:T(8,128)(2,1)S(1)}, u32[]{:S(2)}, u32[]{:S(2)}) collective-permute-start(bf16[96,1280]{1,0:T(8,128)(2,1)S(1)} %shard_map.120.refs_4_), channel_id=1, source_target_pairs={{0,16},{4,20},{8,24},{12,28},{16,0},{20,4},{24,8},{28,12},{1,17},{... | collective-permute-start | bytes 737288 | tf_op jit(solution)/shard_map/ppermute | solution.py:328
  57.1 12.6 %collective-permute-start.33 = (bf16[96,1280]{1,0:T(8,128)(2,1)S(1)}, bf16[96,1280]{1,0:T(8,128)(2,1)S(1)}, u32[]{:S(2)}, u32[]{:S(2)}) collective-permute-start(bf16[96,1280]{1,0:T(8,128)(2,1)S(1)} %get-tuple-element.86.refs_4_.refs_12_), channel_id=1, source_target_pairs={{0,16},{4,20},{8,24},{12,28},{16,0},{20,4},{24,8},{28,12},{1,17},{... | collective-permute-start | bytes 737288 | tf_op jit(solution)/shard_map/ppermute | solution.py:328
  62.7 8.8 %collective-permute-start.35 = (bf16[96,1280]{1,0:T(8,128)(2,1)S(1)}, bf16[96,1280]{1,0:T(8,128)(2,1)S(1)}, u32[]{:S(2)}, u32[]{:S(2)}) collective-permute-start(bf16[96,1280]{1,0:T(8,128)(2,1)S(1)} %get-tuple-element.88.refs_4_.refs_12_), channel_id=1, source_target_pairs={{0,8},{4,12},{8,0},{12,4},{16,24},{20,28},{24,16},{28,20},{1,9},{5... | collective-permute-start | bytes 737288 | tf_op jit(solution)/shard_map/ppermute | solution.py:328
  64.4 11.6 %collective-permute-start.8 = (bf16[96,1280]{1,0:T(8,128)(2,1)S(1)}, bf16[96,1280]{1,0:T(8,128)(2,1)S(1)}, u32[]{:S(2)}, u32[]{:S(2)}) collective-permute-start(bf16[96,1280]{1,0:T(8,128)(2,1)S(1)} %collective-permute-done.7.refs_6_), channel_id=1, source_target_pairs={{0,8},{4,12},{8,0},{12,4},{16,24},{20,28},{24,16},{28,20},{1,9},{5... | collective-permute-start | bytes 737288 | tf_op jit(solution)/shard_map/ppermute | solution.py:328
  69.7 6.6 %collective-permute-start.16 = (bf16[96,1280]{1,0:T(8,128)(2,1)S(1)}, bf16[96,1280]{1,0:T(8,128)(2,1)S(1)}, u32[]{:S(2)}, u32[]{:S(2)}) collective-permute-start(bf16[96,1280]{1,0:T(8,128)(2,1)S(1)} %collective-permute-done.14.refs_5_), channel_id=1, source_target_pairs={{0,16},{4,20},{8,24},{12,28},{16,0},{20,4},{24,8},{28,12},{1,17},{... | collective-permute-start | bytes 737288 | tf_op jit(solution)/shard_map/ppermute | solution.py:328
  71.5 18.1 %collective-permute-start.36 = (bf16[96,1280]{1,0:T(8,128)(2,1)S(1)}, bf16[96,1280]{1,0:T(8,128)(2,1)S(1)}, u32[]{:S(2)}, u32[]{:S(2)}) collective-permute-start(bf16[96,1280]{1,0:T(8,128)(2,1)S(1)} %get-tuple-element.88.refs_4_.refs_12_), channel_id=1, source_target_pairs={{0,16},{4,20},{8,24},{12,28},{16,0},{20,4},{24,8},{28,12},{1,17},{... | collective-permute-start | bytes 737288 | tf_op jit(solution)/shard_map/ppermute | solution.py:328
  76.0 13.5 %collective-permute-start.28 = (bf16[64,1280]{1,0:T(8,128)(2,1)S(1)}, bf16[64,1280]{1,0:T(8,128)(2,1)S(1)}, u32[]{:S(2)}, u32[]{:S(2)}) collective-permute-start(bf16[64,1280]{1,0:T(8,128)(2,1)S(1)} %collective-permute-done.27.refs_2_.refs_10_), channel_id=1, source_target_pairs={{0,8},{4,12},{8,0},{12,4},{16,24},{20,28},{24,16},{28,20},{1,9},{5... | collective-permute-start | bytes 491528 | tf_op jit(solution)/shard_map/ppermute | solution.py:328
  76.3 13.3 %collective-permute-start.37 = (bf16[96,1280]{1,0:T(8,128)(2,1)S(1)}, bf16[96,1280]{1,0:T(8,128)(2,1)S(1)}, u32[]{:S(2)}, u32[]{:S(2)}) collective-permute-start(bf16[96,1280]{1,0:T(8,128)(2,1)S(1)} %collective-permute-done.35.refs_5_.refs_13_), channel_id=1, source_target_pairs={{0,16},{4,20},{8,24},{12,28},{16,0},{20,4},{24,8},{28,12},{1,17},{... | collective-permute-start | bytes 737288 | tf_op jit(solution)/shard_map/ppermute | solution.py:328
  78.7 14.4 %collective-permute-start.32 = (bf16[96,1280]{1,0:T(8,128)(2,1)S(1)}, bf16[96,1280]{1,0:T(8,128)(2,1)S(1)}, u32[]{:S(2)}, u32[]{:S(2)}) collective-permute-start(bf16[96,1280]{1,0:T(8,128)(2,1)S(1)} %get-tuple-element.86.refs_4_.refs_12_), channel_id=1, source_target_pairs={{0,8},{4,12},{8,0},{12,4},{16,24},{20,28},{24,16},{28,20},{1,9},{5... | collective-permute-start | bytes 737288 | tf_op jit(solution)/shard_map/ppermute | solution.py:328
  80.1 13.0 %collective-permute-start.34 = (bf16[96,1280]{1,0:T(8,128)(2,1)S(1)}, bf16[96,1280]{1,0:T(8,128)(2,1)S(1)}, u32[]{:S(2)}, u32[]{:S(2)}) collective-permute-start(bf16[96,1280]{1,0:T(8,128)(2,1)S(1)} %collective-permute-done.33.refs_6_.refs_14_), channel_id=1, source_target_pairs={{0,8},{4,12},{8,0},{12,4},{16,24},{20,28},{24,16},{28,20},{1,9},{5... | collective-permute-start | bytes 737288 | tf_op jit(solution)/shard_map/ppermute | solution.py:328
  89.5 13.9 %collective-permute-start.17 = (bf16[2,64,1280]{2,1,0:T(8,128)(2,1)S(1)}, bf16[2,64,1280]{2,1,0:T(8,128)(2,1)S(1)}, u32[]{:S(2)}, u32[]{:S(2)}) collective-permute-start(bf16[2,64,1280]{2,1,0:T(8,128)(2,1)S(1)} %get-tuple-element.70), channel_id=1, source_target_pairs={{0,16},{4,20},{8,24},{12,28},{16,0},{20,4},{24,8},{28,12},{1,17},{... | collective-permute-start | bytes 983048 | tf_op jit(solution)/shard_map/ppermute | solution.py:328
  96.7 8.2 %collective-permute-start.38 = (bf16[2,64,1280]{2,1,0:T(8,128)(2,1)S(1)}, bf16[2,64,1280]{2,1,0:T(8,128)(2,1)S(1)}, u32[]{:S(2)}, u32[]{:S(2)}) collective-permute-start(bf16[2,64,1280]{2,1,0:T(8,128)(2,1)S(1)} %get-tuple-element.93), channel_id=1, source_target_pairs={{0,8},{4,12},{8,0},{12,4},{16,24},{20,28},{24,16},{28,20},{1,9},{5... | collective-permute-start | bytes 983048 | tf_op jit(solution)/shard_map/ppermute | solution.py:328
  100.2 77.5 %collective-permute-start.50 = (bf16[2,320,1280]{2,1,0:T(8,128)(2,1)S(1)}, bf16[2,320,1280]{2,1,0:T(8,128)(2,1)S(1)}, u32[]{:S(2)}, u32[]{:S(2)}) collective-permute-start(bf16[2,320,1280]{2,1,0:T(8,128)(2,1)S(1)} %get-tuple-element.111), channel_id=1, source_target_pairs={{0,4},{4,0},{8,12},{12,8},{16,20},{20,16},{24,28},{28,24},{1,5},{5... | collective-permute-start | bytes 4915208 | tf_op jit(solution)/shard_map/ppermute | solution.py:328
  102.2 75.6 %collective-permute-start.51 = (bf16[2,320,1280]{2,1,0:T(8,128)(2,1)S(1)}, bf16[2,320,1280]{2,1,0:T(8,128)(2,1)S(1)}, u32[]{:S(2)}, u32[]{:S(2)}) collective-permute-start(bf16[2,320,1280]{2,1,0:T(8,128)(2,1)S(1)} %get-tuple-element.112), channel_id=1, source_target_pairs={{0,4},{4,0},{8,12},{12,8},{16,20},{20,16},{24,28},{28,24},{1,5},{5... | collective-permute-start | bytes 4915208 | tf_op jit(solution)/shard_map/ppermute | solution.py:328
  102.7 17.4 %collective-permute-start.40 = (bf16[2,96,1280]{2,1,0:T(8,128)(2,1)S(1)}, bf16[2,96,1280]{2,1,0:T(8,128)(2,1)S(1)}, u32[]{:S(2)}, u32[]{:S(2)}) collective-permute-start(bf16[2,96,1280]{2,1,0:T(8,128)(2,1)S(1)} %get-tuple-element.95), channel_id=1, source_target_pairs={{0,8},{4,12},{8,0},{12,4},{16,24},{20,28},{24,16},{28,20},{1,9},{5... | collective-permute-start | bytes 1474568 | tf_op jit(solution)/shard_map/ppermute | solution.py:328
  103.4 16.0 %collective-permute-start.18 = (bf16[1,64,1280]{2,1,0:T(8,128)(2,1)S(1)}, bf16[1,64,1280]{2,1,0:T(8,128)(2,1)S(1)}, u32[]{:S(2)}, u32[]{:S(2)}) collective-permute-start(bf16[1,64,1280]{2,1,0:T(8,128)(2,1)S(1)} %shard_map.123), channel_id=1, source_target_pairs={{0,8},{4,12},{8,0},{12,4},{16,24},{20,28},{24,16},{28,20},{1,9},{5... | collective-permute-start | bytes 491528 | tf_op jit(solution)/shard_map/ppermute | solution.py:328
  104.9 17.3 %collective-permute-start.43 = (bf16[2,96,1280]{2,1,0:T(8,128)(2,1)S(1)}, bf16[2,96,1280]{2,1,0:T(8,128)(2,1)S(1)}, u32[]{:S(2)}, u32[]{:S(2)}) collective-permute-start(bf16[2,96,1280]{2,1,0:T(8,128)(2,1)S(1)} %get-tuple-element.98), channel_id=1, source_target_pairs={{0,16},{4,20},{8,24},{12,28},{16,0},{20,4},{24,8},{28,12},{1,17},{... | collective-permute-start | bytes 1474568 | tf_op jit(solution)/shard_map/ppermute | solution.py:328
  119.4 12.3 %collective-permute-start.19 = (bf16[2,96,1280]{2,1,0:T(8,128)(2,1)S(1)}, bf16[2,96,1280]{2,1,0:T(8,128)(2,1)S(1)}, u32[]{:S(2)}, u32[]{:S(2)}) collective-permute-start(bf16[2,96,1280]{2,1,0:T(8,128)(2,1)S(1)} %get-tuple-element.72), channel_id=1, source_target_pairs={{0,8},{4,12},{8,0},{12,4},{16,24},{20,28},{24,16},{28,20},{1,9},{5... | collective-permute-start | bytes 1474568 | tf_op jit(solution)/shard_map/ppermute | solution.py:328
  120.1 14.1 %collective-permute-start.21 = (bf16[2,96,1280]{2,1,0:T(8,128)(2,1)S(1)}, bf16[2,96,1280]{2,1,0:T(8,128)(2,1)S(1)}, u32[]{:S(2)}, u32[]{:S(2)}) collective-permute-start(bf16[2,96,1280]{2,1,0:T(8,128)(2,1)S(1)} %get-tuple-element.74), channel_id=1, source_target_pairs={{0,16},{4,20},{8,24},{12,28},{16,0},{20,4},{24,8},{28,12},{1,17},{... | collective-permute-start | bytes 1474568 | tf_op jit(solution)/shard_map/ppermute | solution.py:328
  122.2 17.3 %collective-permute-start.41 = (bf16[1,96,1280]{2,1,0:T(8,128)(2,1)S(1)}, bf16[1,96,1280]{2,1,0:T(8,128)(2,1)S(1)}, u32[]{:S(2)}, u32[]{:S(2)}) collective-permute-start(bf16[1,96,1280]{2,1,0:T(8,128)(2,1)S(1)} %shard_map.132), channel_id=1, source_target_pairs={{0,16},{4,20},{8,24},{12,28},{16,0},{20,4},{24,8},{28,12},{1,17},{... | collective-permute-start | bytes 737288 | tf_op jit(solution)/shard_map/ppermute | solution.py:328
  131.8 9.1 %collective-permute-start.44 = (bf16[1,96,1280]{2,1,0:T(8,128)(2,1)S(1)}, bf16[1,96,1280]{2,1,0:T(8,128)(2,1)S(1)}, u32[]{:S(2)}, u32[]{:S(2)}) collective-permute-start(bf16[1,96,1280]{2,1,0:T(8,128)(2,1)S(1)} %shard_map.134), channel_id=1, source_target_pairs={{0,8},{4,12},{8,0},{12,4},{16,24},{20,28},{24,16},{28,20},{1,9},{5... | collective-permute-start | bytes 737288 | tf_op jit(solution)/shard_map/ppermute | solution.py:328
  134.2 12.3 %collective-permute-start.20 = (bf16[1,96,1280]{2,1,0:T(8,128)(2,1)S(1)}, bf16[1,96,1280]{2,1,0:T(8,128)(2,1)S(1)}, u32[]{:S(2)}, u32[]{:S(2)}) collective-permute-start(bf16[1,96,1280]{2,1,0:T(8,128)(2,1)S(1)} %shard_map.124), channel_id=1, source_target_pairs={{0,16},{4,20},{8,24},{12,28},{16,0},{20,4},{24,8},{28,12},{1,17},{... | collective-permute-start | bytes 737288 | tf_op jit(solution)/shard_map/ppermute | solution.py:328
  139.5 9.0 %collective-permute-start.22 = (bf16[1,96,1280]{2,1,0:T(8,128)(2,1)S(1)}, bf16[1,96,1280]{2,1,0:T(8,128)(2,1)S(1)}, u32[]{:S(2)}, u32[]{:S(2)}) collective-permute-start(bf16[1,96,1280]{2,1,0:T(8,128)(2,1)S(1)} %shard_map.125), channel_id=1, source_target_pairs={{0,8},{4,12},{8,0},{12,4},{16,24},{20,28},{24,16},{28,20},{1,9},{5... | collective-permute-start | bytes 737288 | tf_op jit(solution)/shard_map/ppermute | solution.py:328
  146.5 6.9 %collective-permute-start.45 = (bf16[32,1280]{1,0:T(8,128)(2,1)S(1)}, bf16[32,1280]{1,0:T(8,128)(2,1)S(1)}, u32[]{:S(2)}, u32[]{:S(2)}) collective-permute-start(bf16[32,1280]{1,0:T(8,128)(2,1)S(1)} %get-tuple-element.99), channel_id=1, source_target_pairs={{0,1},{1,0},{2,3},{3,2},{4,5},{5,4},{6,7},{7,6},{8,9},{9,8},{10,11... | collective-permute-start | bytes 245768 | tf_op jit(solution)/shard_map/ppermute | solution.py:333
  148.5 10.3 %collective-permute-start.46 = (bf16[32,1280]{1,0:T(8,128)(2,1)S(1)}, bf16[32,1280]{1,0:T(8,128)(2,1)S(1)}, u32[]{:S(2)}, u32[]{:S(2)}) collective-permute-start(bf16[32,1280]{1,0:T(8,128)(2,1)S(1)} %get-tuple-element.100), channel_id=1, source_target_pairs={{0,2},{1,3},{2,0},{3,1},{4,6},{5,7},{6,4},{7,5},{8,10},{9,11},{10,... | collective-permute-start | bytes 245768 | tf_op jit(solution)/shard_map/ppermute | solution.py:333
  151.5 9.9 %collective-permute-start.47 = (bf16[32,1280]{1,0:T(8,128)(2,1)S(1)}, bf16[32,1280]{1,0:T(8,128)(2,1)S(1)}, u32[]{:S(2)}, u32[]{:S(2)}) collective-permute-start(bf16[32,1280]{1,0:T(8,128)(2,1)S(1)} %get-tuple-element.101), channel_id=1, source_target_pairs={{0,2},{1,3},{2,0},{3,1},{4,6},{5,7},{6,4},{7,5},{8,10},{9,11},{10,... | collective-permute-start | bytes 245768 | tf_op jit(solution)/shard_map/ppermute | solution.py:333
  153.4 8.1 %collective-permute-start.48 = (bf16[32,1280]{1,0:T(8,128)(2,1)S(1)}, bf16[32,1280]{1,0:T(8,128)(2,1)S(1)}, u32[]{:S(2)}, u32[]{:S(2)}) collective-permute-start(bf16[32,1280]{1,0:T(8,128)(2,1)S(1)} %get-tuple-element.102), channel_id=1, source_target_pairs={{0,3},{1,2},{2,1},{3,0},{4,7},{5,6},{6,5},{7,4},{8,11},{9,10},{10,... | collective-permute-start | bytes 245768 | tf_op jit(solution)/shard_map/ppermute | solution.py:333
  158.8 7.3 %collective-permute-start.49 = (bf16[32,1280]{1,0:T(8,128)(2,1)S(1)}, bf16[32,1280]{1,0:T(8,128)(2,1)S(1)}, u32[]{:S(2)}, u32[]{:S(2)}) collective-permute-start(bf16[32,1280]{1,0:T(8,128)(2,1)S(1)} %get-tuple-element.103), channel_id=1, source_target_pairs={{0,3},{1,2},{2,1},{3,0},{4,7},{5,6},{6,5},{7,4},{8,11},{9,10},{10,... | collective-permute-start | bytes 245768 | tf_op jit(solution)/shard_map/ppermute | solution.py:333
  161.5 8.5 %collective-permute-start.23 = (bf16[64,1280]{1,0:T(8,128)(2,1)S(1)}, bf16[64,1280]{1,0:T(8,128)(2,1)S(1)}, u32[]{:S(2)}, u32[]{:S(2)}) collective-permute-start(bf16[64,1280]{1,0:T(8,128)(2,1)S(1)} %get-tuple-element.75), channel_id=1, source_target_pairs={{0,1},{1,0},{2,3},{3,2},{4,5},{5,4},{6,7},{7,6},{8,9},{9,8},{10,11... | collective-permute-start | bytes 491528 | tf_op jit(solution)/shard_map/ppermute | solution.py:333
  161.5 14.8 %collective-permute-start.24 = (bf16[64,1280]{1,0:T(8,128)(2,1)S(1)}, bf16[64,1280]{1,0:T(8,128)(2,1)S(1)}, u32[]{:S(2)}, u32[]{:S(2)}) collective-permute-start(bf16[64,1280]{1,0:T(8,128)(2,1)S(1)} %get-tuple-element.76), channel_id=1, source_target_pairs={{0,2},{1,3},{2,0},{3,1},{4,6},{5,7},{6,4},{7,5},{8,10},{9,11},{10,... | collective-permute-start | bytes 491528 | tf_op jit(solution)/shard_map/ppermute | solution.py:333
  166.1 10.2 %collective-permute-start.25 = (bf16[64,1280]{1,0:T(8,128)(2,1)S(1)}, bf16[64,1280]{1,0:T(8,128)(2,1)S(1)}, u32[]{:S(2)}, u32[]{:S(2)}) collective-permute-start(bf16[64,1280]{1,0:T(8,128)(2,1)S(1)} %get-tuple-element.77), channel_id=1, source_target_pairs={{0,3},{1,2},{2,1},{3,0},{4,7},{5,6},{6,5},{7,4},{8,11},{9,10},{10,... | collective-permute-start | bytes 491528 | tf_op jit(solution)/shard_map/ppermute | solution.py:333
  (9 other events, 156.7 us)
where the time goes:
time: 180 us
  waiting for transfers between devices  87.7 us (49%)
  starting transfers between devices  63.8 us (35%)
  Pallas kernels  26.3 us (15%)
    ppermute x34, waiting for transfers between devices, swap(): return lax.ppermute(values, 'dp', [(i, i ^ mask) for i in range(groups)])  58.6 us
    ppermute x34, starting transfers between devices, swap(): return lax.ppermute(values, 'dp', [(i, i ^ mask) for i in range(groups)])  35.5 us
    ppermute x18, waiting for transfers between devices, cross(): lax.ppermute(piece, 'expert', [(i, i ^ s) for i in range(planes)])  29.1 us
    ppermute x18, starting transfers between devices, cross(): lax.ppermute(piece, 'expert', [(i, i ^ s) for i in range(planes)])  28.3 us
    pallas_call x21, Pallas kernels, run(): pl.pallas_call(kernel, out_shape=outs, grid=(1,), in_specs=specs, out_spe...  24.2 us
  transfers between devices with their start and end apart: 52, of which 24 were waited for; matrix products, arithmetic and copies ran while one was open for 0% of the time, Pallas kernels for 13%

commit v1 on v0

--- a/solution.py
+++ b/solution.py
@@ -171,7 +171,8 @@
     half = 0.5 * (1.0 + lax.erf(pre * root_half))
     hidden = (pre * half).astype(jnp.bfloat16)
     hidden_ref[...] = hidden
-    slope_ref[...] = half + pre * jnp.exp(-0.5 * pre * pre) * density_scale
+    slope = half + pre * jnp.exp(-0.5 * pre * pre) * density_scale
+    slope_ref[...] = slope.astype(slope_ref.dtype)
     down = jnp.concatenate([down_own[0], down_pair[0]], 0)
     spread(dot(hidden, down, 1, 0), blocks, parts, held_refs, outs)
 
@@ -196,7 +197,7 @@
     held_refs = refs[2 * blocks + 5 : 2 * blocks + 5 + held]
     dpre_ref, *outs = refs[2 * blocks + 5 + held :]
     down = jnp.concatenate([down_own[0], down_pair[0]], 0)
-    dpre = (dot(grads, down, 1, 1) * slope_ref[...]).astype(jnp.bfloat16)
+    dpre = (dot(grads, down, 1, 1) * slope_ref[...].astype(jnp.float32)).astype(jnp.bfloat16)
     dpre_ref[...] = dpre
     up = jnp.concatenate([up_own[0], up_pair[0]], 0)
     spread(dot(dpre, up, 1, 0), blocks, parts, held_refs, outs)
@@ -433,7 +434,6 @@
 
     rows = blocks * block_rows
     flat = ((rows, 2 * units), low)
-    wide = ((rows, 2 * units), jnp.float32)
 
     def outs_of(l, parts):
         sizes = [(l + 1) * cap] + [stop - start for start, stop, _ in parts[1:]]
@@ -447,7 +447,7 @@
             features[l]
             + [(expand_weight, l), (up_pair, l), (reduce_weight, l), (down_pair, l)]
             + held,
-            [flat, wide] + outs_of(l, parts),
+            [flat, flat] + outs_of(l, parts),
         )
         hiddens.append(hidden)
         slopes.append(slope)

time: 180 us -> 181 us (level)
  starting transfers between devices: 63.8 us -> 66.7 us
  waiting for transfers between devices: 87.7 us -> 84.9 us
    ppermute x18, starting transfers between devices: 28.3 us -> 31.1 us  [cross(): lax.ppermute(piece, 'expert', [(i, i ^ s) for i in range(planes)])]
    ppermute x18, waiting for transfers between devices: 29.1 us -> 26.3 us  [cross(): lax.ppermute(piece, 'expert', [(i, i ^ s) for i in range(planes)])]
  transfers between devices with their start and end apart: 52 -> 52, of which waited for: 24 -> 23; matrix products, arithmetic and copies ran while one was open for 0% -> 0% of each run, Pallas kernels for 13% -> 13%
where the time goes in v1:
time: 181 us; the launch traced here: 180 us
  waiting for transfers between devices  84.9 us (47%)
  starting transfers between devices  66.7 us (37%)
  Pallas kernels  26.3 us (15%)
    ppermute x34, waiting for transfers between devices, swap(): return lax.ppermute(values, 'dp', [(i, i ^ mask) for i in range(groups)])  58.6 us
    ppermute x34, starting transfers between devices, swap(): return lax.ppermute(values, 'dp', [(i, i ^ mask) for i in range(groups)])  35.5 us
    ppermute x18, starting transfers between devices, cross(): lax.ppermute(piece, 'expert', [(i, i ^ s) for i in range(planes)])  31.1 us
    ppermute x18, waiting for transfers between devices, cross(): lax.ppermute(piece, 'expert', [(i, i ^ s) for i in range(planes)])  26.3 us
    pallas_call x21, Pallas kernels, run(): pl.pallas_call(kernel, out_shape=outs, grid=(1,), in_specs=specs, out_spe...  24.2 us
  transfers between devices with their start and end apart: 52, of which 23 were waited for; matrix products, arithmetic and copies ran while one was open for 0% of the time, Pallas kernels for 13%

profile of v1, /device:TPU:0, one launch (start us, length us, event | category | flops | bytes accessed | tf_op | source)
XLA Modules:
  0.0 180.2 jit_solution(6959226570738034268)
XLA Ops:
  1.3 2.1 %route.1 = (bf16[64,1280]{1,0:T(8,128)(2,1)S(1)}, bf16[64,1280]{1,0:T(8,128)(2,1)S(1)}, bf16[32,1280]{1,0:T(8,128)(2,1)S(1)}, bf16[32,1280]{1,0:T(8,128)(2,1)S(1...) custom-call(s32[1]{0:T(128)} %bitcast.me_ref, ...), custom_call_target="tpu_custom_call" | custom-call | tf_op jit(solution)/shard_map/route/pallas_call | solution.py:380
  3.4 3.1 %collective-permute-start.3 = (bf16[32,1280]{1,0:T(8,128)(2,1)S(1)}, bf16[32,1280]{1,0:T(8,128)(2,1)S(1)}, u32[]{:S(2)}, u32[]{:S(2)}) collective-permute-start(bf16[32,1280]{1,0:T(8,128)(2,1)S(1)} %get-tuple-element.61), channel_id=1, source_target_pairs={{0,1},{1,0},{2,3},{3,2},{4,5},{5,4},{6,7},{7,6},{8,9},{9,8},{10,11... | collective-permute-start | bytes 245768 | tf_op jit(solution)/shard_map/ppermute | solution.py:334
  6.4 2.6 %collective-permute-start.4 = (bf16[32,1280]{1,0:T(8,128)(2,1)S(1)}, bf16[32,1280]{1,0:T(8,128)(2,1)S(1)}, u32[]{:S(2)}, u32[]{:S(2)}) collective-permute-start(bf16[32,1280]{1,0:T(8,128)(2,1)S(1)} %get-tuple-element.62), channel_id=1, source_target_pairs={{0,2},{1,3},{2,0},{3,1},{4,6},{5,7},{6,4},{7,5},{8,10},{9,11},{10,... | collective-permute-start | bytes 245768 | tf_op jit(solution)/shard_map/ppermute | solution.py:334
  9.1 1.8 collective-permute-start.11
  10.9 5.0 %collective-permute-done.4.refs_1_ = bf16[32,1280]{1,0:T(8,128)(2,1)S(1)} collective-permute-done((bf16[32,1280]{1,0:T(8,128)(2,1)S(1)}, bf16[32,1280]{1,0:T(8,128)(2,1)S(1)}, u32[]{:S(2)}, u32[]{:S(2)}) %collective-permute-start.4) | collective-permute-done | bytes 81952 | tf_op jit(solution)/shard_map/ppermute | solution.py:334
  15.9 1.5 collective-permute-start
  18.3 1.6 collective-permute-start.13
  19.9 5.0 %collective-permute-done.12.refs_1_ = bf16[32,1280]{1,0:T(8,128)(2,1)S(1)} collective-permute-done((bf16[32,1280]{1,0:T(8,128)(2,1)S(1)}, bf16[32,1280]{1,0:T(8,128)(2,1)S(1)}, u32[]{:S(2)}, u32[]{:S(2)}) %collective-permute-start.12) | collective-permute-done | bytes 81952 | tf_op jit(solution)/shard_map/ppermute | solution.py:334
  24.9 1.5 collective-permute-start.1
  27.7 2.6 %collective-permute-done.1.refs_2_ = bf16[64,1280]{1,0:T(8,128)(2,1)S(1)} collective-permute-done((bf16[64,1280]{1,0:T(8,128)(2,1)S(1)}, bf16[64,1280]{1,0:T(8,128)(2,1)S(1)}, u32[]{:S(2)}, u32[]{:S(2)}) %collective-permute-start.1) | collective-permute-done | bytes 163872 | tf_op jit(solution)/shard_map/ppermute | solution.py:329
  30.3 1.5 collective-permute-done.26.refs_1_.refs_9_
  32.6 2.4 %collective-permute-start.31 = (bf16[64,1280]{1,0:T(8,128)(2,1)S(1)}, bf16[64,1280]{1,0:T(8,128)(2,1)S(1)}, u32[]{:S(2)}, u32[]{:S(2)}) collective-permute-start(bf16[64,1280]{1,0:T(8,128)(2,1)S(1)} %get-tuple-element.85), channel_id=1, source_target_pairs={{0,3},{1,2},{2,1},{3,0},{4,7},{5,6},{6,5},{7,4},{8,11},{9,10},{10,... | collective-permute-start | bytes 491528 | tf_op jit(solution)/shard_map/ppermute | solution.py:334
  35.0 2.3 %collective-permute-done.29.refs_0_ = bf16[64,1280]{1,0:T(8,128)(2,1)S(1)} collective-permute-done((bf16[64,1280]{1,0:T(8,128)(2,1)S(1)}, bf16[64,1280]{1,0:T(8,128)(2,1)S(1)}, u32[]{:S(2)}, u32[]{:S(2)}) %collective-permute-start.29) | collective-permute-done | bytes 163872 | tf_op jit(solution)/shard_map/ppermute | solution.py:334
  37.4 1.5 collective-permute-start.6
  38.9 3.5 %collective-permute-done.30.refs_1_ = bf16[64,1280]{1,0:T(8,128)(2,1)S(1)} collective-permute-done((bf16[64,1280]{1,0:T(8,128)(2,1)S(1)}, bf16[64,1280]{1,0:T(8,128)(2,1)S(1)}, u32[]{:S(2)}, u32[]{:S(2)}) %collective-permute-start.30) | collective-permute-done | bytes 163872 | tf_op jit(solution)/shard_map/ppermute | solution.py:334
  44.5 10.2 %collective-permute-done.2.refs_3_ = bf16[64,1280]{1,0:T(8,128)(2,1)S(1)} collective-permute-done((bf16[64,1280]{1,0:T(8,128)(2,1)S(1)}, bf16[64,1280]{1,0:T(8,128)(2,1)S(1)}, u32[]{:S(2)}, u32[]{:S(2)}) %collective-permute-start.2) | collective-permute-done | bytes 163872 | tf_op jit(solution)/shard_map/ppermute | solution.py:329
  55.6 1.5 collective-permute-start.15
  57.6 5.1 %collective-permute-done.14.refs_5_ = bf16[96,1280]{1,0:T(8,128)(2,1)S(1)} collective-permute-done((bf16[96,1280]{1,0:T(8,128)(2,1)S(1)}, bf16[96,1280]{1,0:T(8,128)(2,1)S(1)}, u32[]{:S(2)}, u32[]{:S(2)}) %collective-permute-start.14) | collective-permute-done | bytes 245792 | tf_op jit(solution)/shard_map/ppermute | solution.py:329
  65.6 4.1 %collective-permute-done.33.refs_6_.refs_14_ = bf16[96,1280]{1,0:T(8,128)(2,1)S(1)} collective-permute-done((bf16[96,1280]{1,0:T(8,128)(2,1)S(1)}, bf16[96,1280]{1,0:T(8,128)(2,1)S(1)}, u32[]{:S(2)}, u32[]{:S(2)}) %collective-permute-start.33) | collective-permute-done | bytes 245792 | tf_op jit(solution)/shard_map/ppermute | solution.py:329
  69.7 1.5 collective-permute-start.16
  72.3 3.6 %collective-permute-done.8.refs_7_ = bf16[96,1280]{1,0:T(8,128)(2,1)S(1)} collective-permute-done((bf16[96,1280]{1,0:T(8,128)(2,1)S(1)}, bf16[96,1280]{1,0:T(8,128)(2,1)S(1)}, u32[]{:S(2)}, u32[]{:S(2)}) %collective-permute-start.8) | collective-permute-done | bytes 245792 | tf_op jit(solution)/shard_map/ppermute | solution.py:329
  76.3 2.5 %collective-permute-start.37 = (bf16[96,1280]{1,0:T(8,128)(2,1)S(1)}, bf16[96,1280]{1,0:T(8,128)(2,1)S(1)}, u32[]{:S(2)}, u32[]{:S(2)}) collective-permute-start(bf16[96,1280]{1,0:T(8,128)(2,1)S(1)} %collective-permute-done.35.refs_5_.refs_13_), channel_id=1, source_target_pairs={{0,16},{4,20},{8,24},{12,28},{16,0},{20,4},{24,8},{28,12},{1,17},{... | collective-permute-start | bytes 737288 | tf_op jit(solution)/shard_map/ppermute | solution.py:329
  82.2 3.7 %shard_map.121 = (bf16[512,640]{1,0:T(8,128)(2,1)S(1)}, bf16[512,640]{1,0:T(8,128)(2,1)S(1)}, bf16[2,32,1280]{2,1,0:T(8,128)(2,1)S(1)}, bf16[2,32,1280]{2,1,0:T(...) custom-call(bf16[64,1280]{1,0:T(8,128)(2,1)S(1)} %get-tuple-element.60.refs_0_, ...), custom_call_target="tpu_custom_call" | custom-call | tf_op jit(solution)/shard_map/pallas_call | solution.py:304
  85.9 3.6 %shard_map.122 = (bf16[512,640]{1,0:T(8,128)(2,1)S(1)}, bf16[512,640]{1,0:T(8,128)(2,1)S(1)}, bf16[2,64,1280]{2,1,0:T(8,128)(2,1)S(1)}, bf16[2,64,1280]{2,1,0:T(...) custom-call(bf16[64,1280]{1,0:T(8,128)(2,1)S(1)} %get-tuple-element.60.refs_0_, ...), custom_call_target="tpu_custom_call" | custom-call | tf_op jit(solution)/shard_map/pallas_call | solution.py:304
  89.6 3.5 %shard_map.129 = (bf16[512,640]{1,0:T(8,128)(2,1)S(1)}, bf16[2,32,1280]{2,1,0:T(8,128)(2,1)S(1)}, bf16[2,32,1280]{2,1,0:T(8,128)(2,1)S(1)}, bf16[2,96,1280]{2,1,0:T(8,128)(2,1)S(1)}, bf16[2,96,1280]{2,1,0:T(8,128)(2,1)S(1)}) custom-call(bf16[64,1280]{1,0:T(8,128)(2,1)S(1)} %get-tuple-element.82.refs_0_.refs_8_, ...), custom_call_target="tpu_custom_call" | custom-call | tf_op jit(solution)/shard_map/pallas_call | solution.py:304
  93.1 3.5 %shard_map.130 = (bf16[512,640]{1,0:T(8,128)(2,1)S(1)}, bf16[2,64,1280]{2,1,0:T(8,128)(2,1)S(1)}, bf16[2,64,1280]{2,1,0:T(8,128)(2,1)S(1)}, bf16[2,96,1280]{2,1,0:T(8,128)(2,1)S(1)}, bf16[2,96,1280]{2,1,0:T(8,128)(2,1)S(1)}) custom-call(bf16[64,1280]{1,0:T(8,128)(2,1)S(1)} %get-tuple-element.82.refs_0_.refs_8_, ...), custom_call_target="tpu_custom_call" | custom-call | tf_op jit(solution)/shard_map/pallas_call | solution.py:304
  98.1 2.1 %shard_map.137 = (bf16[2,320,1280]{2,1,0:T(8,128)(2,1)S(1)}, bf16[2,320,1280]{2,1,0:T(8,128)(2,1)S(1)}) custom-call(bf16[64,1280]{1,0:T(8,128)(2,1)S(1)} %get-tuple-element.60.refs_0_, bf16[64,1280]{1,0:T(8,128)(2,1)S(1)} %collective-permute-done.refs_1_, bf16[64,1280]{1,0:T(8,128)(2,1)S(1)} %collective-permute-done.1.refs_2_, ...), custom_call_target="tpu_custom_call" | custom-call | tf_op jit(solution)/shard_map/pallas_call | solution.py:304
  100.3 1.9 %shard_map.138 = (bf16[2,320,1280]{2,1,0:T(8,128)(2,1)S(1)}, bf16[2,320,1280]{2,1,0:T(8,128)(2,1)S(1)}) custom-call(bf16[64,1280]{1,0:T(8,128)(2,1)S(1)} %get-tuple-element.60.refs_0_, bf16[64,1280]{1,0:T(8,128)(2,1)S(1)} %collective-permute-done.refs_1_, bf16[64,1280]{1,0:T(8,128)(2,1)S(1)} %collective-permute-done.1.refs_2_, ...), custom_call_target="tpu_custom_call" | custom-call | tf_op jit(solution)/shard_map/pallas_call | solution.py:304
  104.9 2.0 %collective-permute-start.43 = (bf16[2,96,1280]{2,1,0:T(8,128)(2,1)S(1)}, bf16[2,96,1280]{2,1,0:T(8,128)(2,1)S(1)}, u32[]{:S(2)}, u32[]{:S(2)}) collective-permute-start(bf16[2,96,1280]{2,1,0:T(8,128)(2,1)S(1)} %get-tuple-element.98), channel_id=1, source_target_pairs={{0,16},{4,20},{8,24},{12,28},{16,0},{20,4},{24,8},{28,12},{1,17},{... | collective-permute-start | bytes 1474568 | tf_op jit(solution)/shard_map/ppermute | solution.py:329
  106.9 12.6 %collective-permute-done.18.refs_2_ = bf16[1,64,1280]{2,1,0:T(8,128)(2,1)S(1)} collective-permute-done((bf16[1,64,1280]{2,1,0:T(8,128)(2,1)S(1)}, bf16[1,64,1280]{2,1,0:T(8,128)(2,1)S(1)}, u32[]{:S(2)}, u32[]{:S(2)}) %collective-permute-start.18) | collective-permute-done | bytes 163872 | tf_op jit(solution)/shard_map/ppermute | solution.py:329
  120.1 2.0 %collective-permute-start.21 = (bf16[2,96,1280]{2,1,0:T(8,128)(2,1)S(1)}, bf16[2,96,1280]{2,1,0:T(8,128)(2,1)S(1)}, u32[]{:S(2)}, u32[]{:S(2)}) collective-permute-start(bf16[2,96,1280]{2,1,0:T(8,128)(2,1)S(1)} %get-tuple-element.74), channel_id=1, source_target_pairs={{0,16},{4,20},{8,24},{12,28},{16,0},{20,4},{24,8},{28,12},{1,17},{... | collective-permute-start | bytes 1474568 | tf_op jit(solution)/shard_map/ppermute | solution.py:329
  122.3 9.5 %collective-permute-done.19.refs_1_ = bf16[2,96,1280]{2,1,0:T(8,128)(2,1)S(1)} collective-permute-done((bf16[2,96,1280]{2,1,0:T(8,128)(2,1)S(1)}, bf16[2,96,1280]{2,1,0:T(8,128)(2,1)S(1)}, u32[]{:S(2)}, u32[]{:S(2)}) %collective-permute-start.19) | collective-permute-done | bytes 491552 | tf_op jit(solution)/shard_map/ppermute | solution.py:329
  132.5 1.7 collective-permute-done.21.refs_1_.refs_4_
  134.2 2.0 %collective-permute-start.20 = (bf16[1,96,1280]{2,1,0:T(8,128)(2,1)S(1)}, bf16[1,96,1280]{2,1,0:T(8,128)(2,1)S(1)}, u32[]{:S(2)}, u32[]{:S(2)}) collective-permute-start(bf16[1,96,1280]{2,1,0:T(8,128)(2,1)S(1)} %shard_map.124), channel_id=1, source_target_pairs={{0,16},{4,20},{8,24},{12,28},{16,0},{20,4},{24,8},{28,12},{1,17},{... | collective-permute-start | bytes 737288 | tf_op jit(solution)/shard_map/ppermute | solution.py:329
  136.2 3.2 %collective-permute-done.41.refs_2_ = bf16[1,96,1280]{2,1,0:T(8,128)(2,1)S(1)} collective-permute-done((bf16[1,96,1280]{2,1,0:T(8,128)(2,1)S(1)}, bf16[1,96,1280]{2,1,0:T(8,128)(2,1)S(1)}, u32[]{:S(2)}, u32[]{:S(2)}) %collective-permute-start.41) | collective-permute-done | bytes 245792 | tf_op jit(solution)/shard_map/ppermute | solution.py:329
  140.9 2.1 %collective-permute-start.39 = (bf16[1,64,1280]{2,1,0:T(8,128)(2,1)S(1)}, bf16[1,64,1280]{2,1,0:T(8,128)(2,1)S(1)}, u32[]{:S(2)}, u32[]{:S(2)}) collective-permute-start(bf16[1,64,1280]{2,1,0:T(8,128)(2,1)S(1)} %shard_map.131), channel_id=1, source_target_pairs={{0,16},{4,20},{8,24},{12,28},{16,0},{20,4},{24,8},{28,12},{1,17},{... | collective-permute-start | bytes 491528 | tf_op jit(solution)/shard_map/ppermute | solution.py:329
  143.2 3.3 %collective-permute-done.39.refs_2_ = bf16[1,64,1280]{2,1,0:T(8,128)(2,1)S(1)} collective-permute-done((bf16[1,64,1280]{2,1,0:T(8,128)(2,1)S(1)}, bf16[1,64,1280]{2,1,0:T(8,128)(2,1)S(1)}, u32[]{:S(2)}, u32[]{:S(2)}) %collective-permute-start.39) | collective-permute-done | bytes 163872 | tf_op jit(solution)/shard_map/ppermute | solution.py:329
  146.5 2.0 %collective-permute-start.45 = (bf16[32,1280]{1,0:T(8,128)(2,1)S(1)}, bf16[32,1280]{1,0:T(8,128)(2,1)S(1)}, u32[]{:S(2)}, u32[]{:S(2)}) collective-permute-start(bf16[32,1280]{1,0:T(8,128)(2,1)S(1)} %get-tuple-element.99), channel_id=1, source_target_pairs={{0,1},{1,0},{2,3},{3,2},{4,5},{5,4},{6,7},{7,6},{8,9},{9,8},{10,11... | collective-permute-start | bytes 245768 | tf_op jit(solution)/shard_map/ppermute | solution.py:334
  148.5 1.7 collective-permute-start.46
  151.5 1.9 %collective-permute-start.47 = (bf16[32,1280]{1,0:T(8,128)(2,1)S(1)}, bf16[32,1280]{1,0:T(8,128)(2,1)S(1)}, u32[]{:S(2)}, u32[]{:S(2)}) collective-permute-start(bf16[32,1280]{1,0:T(8,128)(2,1)S(1)} %get-tuple-element.101), channel_id=1, source_target_pairs={{0,2},{1,3},{2,0},{3,1},{4,6},{5,7},{6,4},{7,5},{8,10},{9,11},{10,... | collective-permute-start | bytes 245768 | tf_op jit(solution)/shard_map/ppermute | solution.py:334
  153.4 2.6 %collective-permute-start.48 = (bf16[32,1280]{1,0:T(8,128)(2,1)S(1)}, bf16[32,1280]{1,0:T(8,128)(2,1)S(1)}, u32[]{:S(2)}, u32[]{:S(2)}) collective-permute-start(bf16[32,1280]{1,0:T(8,128)(2,1)S(1)} %get-tuple-element.102), channel_id=1, source_target_pairs={{0,3},{1,2},{2,1},{3,0},{4,7},{5,6},{6,5},{7,4},{8,11},{9,10},{10,... | collective-permute-start | bytes 245768 | tf_op jit(solution)/shard_map/ppermute | solution.py:334
  156.0 2.8 %collective-permute-done.46.refs_5_ = bf16[32,1280]{1,0:T(8,128)(2,1)S(1)} collective-permute-done((bf16[32,1280]{1,0:T(8,128)(2,1)S(1)}, bf16[32,1280]{1,0:T(8,128)(2,1)S(1)}, u32[]{:S(2)}, u32[]{:S(2)}) %collective-permute-start.46) | collective-permute-done | bytes 81952 | tf_op jit(solution)/shard_map/ppermute | solution.py:334
  158.8 2.1 %collective-permute-start.49 = (bf16[32,1280]{1,0:T(8,128)(2,1)S(1)}, bf16[32,1280]{1,0:T(8,128)(2,1)S(1)}, u32[]{:S(2)}, u32[]{:S(2)}) collective-permute-start(bf16[32,1280]{1,0:T(8,128)(2,1)S(1)} %get-tuple-element.103), channel_id=1, source_target_pairs={{0,3},{1,2},{2,1},{3,0},{4,7},{5,6},{6,5},{7,4},{8,11},{9,10},{10,... | collective-permute-start | bytes 245768 | tf_op jit(solution)/shard_map/ppermute | solution.py:334
  161.5 6.1 %collective-permute-start.24 = (bf16[64,1280]{1,0:T(8,128)(2,1)S(1)}, bf16[64,1280]{1,0:T(8,128)(2,1)S(1)}, u32[]{:S(2)}, u32[]{:S(2)}) collective-permute-start(bf16[64,1280]{1,0:T(8,128)(2,1)S(1)} %get-tuple-element.76), channel_id=1, source_target_pairs={{0,2},{1,3},{2,0},{3,1},{4,6},{5,7},{6,4},{7,5},{8,10},{9,11},{10,... | collective-permute-start | bytes 491528 | tf_op jit(solution)/shard_map/ppermute | solution.py:334
  167.6 1.5 collective-permute-start.25
  170.7 5.6 %collective-permute-done.24.refs_4_ = bf16[64,1280]{1,0:T(8,128)(2,1)S(1)} collective-permute-done((bf16[64,1280]{1,0:T(8,128)(2,1)S(1)}, bf16[64,1280]{1,0:T(8,128)(2,1)S(1)}, u32[]{:S(2)}, u32[]{:S(2)}) %collective-permute-start.24) | collective-permute-done | bytes 163872 | tf_op jit(solution)/shard_map/ppermute | solution.py:334
  176.4 1.4 shard_map.127
  177.8 2.4 %shard_map.139 = (bf16[2,320,1280]{2,1,0:T(8,128)(2,1)}, bf16[2,320,1280]{2,1,0:T(8,128)(2,1)}) custom-call(bf16[2,320,1280]{2,1,0:T(8,128)(2,1)S(1)} %get-tuple-element.107.refs_0_, bf16[2,320,1280]{2,1,0:T(8,128)(2,1)S(1)} %get-tuple-element.110.refs_1_, bf16[2,320,1280]{2,1,0:T(8,128)(2,1)S(1)} %collective-permute-done.50.refs_2_, ...), custom_call_target="tpu_custom_call" | custom-call | tf_op jit(solution)/shard_map/pallas_call | solution.py:304
  (88 shorter events, 26.1 us)
Async XLA Ops:
  0.6 78.1 %collective-permute-start.9 = (bf16[2,320,1280]{2,1,0:T(8,128)(2,1)}, bf16[2,320,1280]{2,1,0:T(8,128)(2,1)S(1)}, u32[]{:S(2)}, u32[]{:S(2)}) collective-permute-start(bf16[2,320,1280]{2,1,0:T(8,128)(2,1)} %refs_8_.7), channel_id=1, source_target_pairs={{0,4},{4,0},{8,12},{12,8},{16,20},{20,16},{24,28},{28,24},{1,5},{5... | collective-permute-start | bytes 4915208 | tf_op jit(solution)/shard_map/ppermute | solution.py:329
  1.2 78.9 %collective-permute-start.10 = (bf16[2,320,1280]{2,1,0:T(8,128)(2,1)}, bf16[2,320,1280]{2,1,0:T(8,128)(2,1)}, u32[]{:S(2)}, u32[]{:S(2)}) collective-permute-start(bf16[2,320,1280]{2,1,0:T(8,128)(2,1)} %refs_10_.8), channel_id=1, source_target_pairs={{0,4},{4,0},{8,12},{12,8},{16,20},{20,16},{24,28},{28,24},{1,5},{5... | collective-permute-start | bytes 4915208 | tf_op jit(solution)/shard_map/ppermute | solution.py:329
  3.4 5.7 %collective-permute-start.3 = (bf16[32,1280]{1,0:T(8,128)(2,1)S(1)}, bf16[32,1280]{1,0:T(8,128)(2,1)S(1)}, u32[]{:S(2)}, u32[]{:S(2)}) collective-permute-start(bf16[32,1280]{1,0:T(8,128)(2,1)S(1)} %get-tuple-element.61), channel_id=1, source_target_pairs={{0,1},{1,0},{2,3},{3,2},{4,5},{5,4},{6,7},{7,6},{8,9},{9,8},{10,11... | collective-permute-start | bytes 245768 | tf_op jit(solution)/shard_map/ppermute | solution.py:334
  6.4 9.4 %collective-permute-start.4 = (bf16[32,1280]{1,0:T(8,128)(2,1)S(1)}, bf16[32,1280]{1,0:T(8,128)(2,1)S(1)}, u32[]{:S(2)}, u32[]{:S(2)}) collective-permute-start(bf16[32,1280]{1,0:T(8,128)(2,1)S(1)} %get-tuple-element.62), channel_id=1, source_target_pairs={{0,2},{1,3},{2,0},{3,1},{4,6},{5,7},{6,4},{7,5},{8,10},{9,11},{10,... | collective-permute-start | bytes 245768 | tf_op jit(solution)/shard_map/ppermute | solution.py:334
  9.0 8.3 %collective-permute-start.5 = (bf16[32,1280]{1,0:T(8,128)(2,1)S(1)}, bf16[32,1280]{1,0:T(8,128)(2,1)S(1)}, u32[]{:S(2)}, u32[]{:S(2)}) collective-permute-start(bf16[32,1280]{1,0:T(8,128)(2,1)S(1)} %get-tuple-element.63), channel_id=1, source_target_pairs={{0,3},{1,2},{2,1},{3,0},{4,7},{5,6},{6,5},{7,4},{8,11},{9,10},{10,... | collective-permute-start | bytes 245768 | tf_op jit(solution)/shard_map/ppermute | solution.py:334
  9.1 9.2 %collective-permute-start.11 = (bf16[32,1280]{1,0:T(8,128)(2,1)S(1)}, bf16[32,1280]{1,0:T(8,128)(2,1)S(1)}, u32[]{:S(2)}, u32[]{:S(2)}) collective-permute-start(bf16[32,1280]{1,0:T(8,128)(2,1)S(1)} %get-tuple-element.64), channel_id=1, source_target_pairs={{0,1},{1,0},{2,3},{3,2},{4,5},{5,4},{6,7},{7,6},{8,9},{9,8},{10,11... | collective-permute-start | bytes 245768 | tf_op jit(solution)/shard_map/ppermute | solution.py:334
  15.9 10.7 %collective-permute-start = (bf16[64,1280]{1,0:T(8,128)(2,1)S(1)}, bf16[64,1280]{1,0:T(8,128)(2,1)S(1)}, u32[]{:S(2)}, u32[]{:S(2)}) collective-permute-start(bf16[64,1280]{1,0:T(8,128)(2,1)S(1)} %get-tuple-element.60.refs_0_), channel_id=1, source_target_pairs={{0,8},{4,12},{8,0},{12,4},{16,24},{20,28},{24,16},{28,20},{1,9},{5... | collective-permute-start | bytes 491528 | tf_op jit(solution)/shard_map/ppermute | solution.py:329
  17.4 7.5 %collective-permute-start.12 = (bf16[32,1280]{1,0:T(8,128)(2,1)S(1)}, bf16[32,1280]{1,0:T(8,128)(2,1)S(1)}, u32[]{:S(2)}, u32[]{:S(2)}) collective-permute-start(bf16[32,1280]{1,0:T(8,128)(2,1)S(1)} %get-tuple-element.65), channel_id=1, source_target_pairs={{0,2},{1,3},{2,0},{3,1},{4,6},{5,7},{6,4},{7,5},{8,10},{9,11},{10,... | collective-permute-start | bytes 245768 | tf_op jit(solution)/shard_map/ppermute | solution.py:334
  18.3 8.1 %collective-permute-start.13 = (bf16[32,1280]{1,0:T(8,128)(2,1)S(1)}, bf16[32,1280]{1,0:T(8,128)(2,1)S(1)}, u32[]{:S(2)}, u32[]{:S(2)}) collective-permute-start(bf16[32,1280]{1,0:T(8,128)(2,1)S(1)} %get-tuple-element.66), channel_id=1, source_target_pairs={{0,3},{1,2},{2,1},{3,0},{4,7},{5,6},{6,5},{7,4},{8,11},{9,10},{10,... | collective-permute-start | bytes 245768 | tf_op jit(solution)/shard_map/ppermute | solution.py:334
  26.5 6.0 %collective-permute-start.27 = (bf16[64,1280]{1,0:T(8,128)(2,1)S(1)}, bf16[64,1280]{1,0:T(8,128)(2,1)S(1)}, u32[]{:S(2)}, u32[]{:S(2)}) collective-permute-start(bf16[64,1280]{1,0:T(8,128)(2,1)S(1)} %get-tuple-element.82.refs_0_.refs_8_), channel_id=1, source_target_pairs={{0,16},{4,20},{8,24},{12,28},{16,0},{20,4},{24,8},{28,12},{1,17},{... | collective-permute-start | bytes 491528 | tf_op jit(solution)/shard_map/ppermute | solution.py:329
  30.3 7.1 %collective-permute-start.29 = (bf16[64,1280]{1,0:T(8,128)(2,1)S(1)}, bf16[64,1280]{1,0:T(8,128)(2,1)S(1)}, u32[]{:S(2)}, u32[]{:S(2)}) collective-permute-start(bf16[64,1280]{1,0:T(8,128)(2,1)S(1)} %get-tuple-element.83), channel_id=1, source_target_pairs={{0,1},{1,0},{2,3},{3,2},{4,5},{5,4},{6,7},{7,6},{8,9},{9,8},{10,11... | collective-permute-start | bytes 491528 | tf_op jit(solution)/shard_map/ppermute | solution.py:334
  31.7 10.6 %collective-permute-start.30 = (bf16[64,1280]{1,0:T(8,128)(2,1)S(1)}, bf16[64,1280]{1,0:T(8,128)(2,1)S(1)}, u32[]{:S(2)}, u32[]{:S(2)}) collective-permute-start(bf16[64,1280]{1,0:T(8,128)(2,1)S(1)} %get-tuple-element.84), channel_id=1, source_target_pairs={{0,2},{1,3},{2,0},{3,1},{4,6},{5,7},{6,4},{7,5},{8,10},{9,11},{10,... | collective-permute-start | bytes 491528 | tf_op jit(solution)/shard_map/ppermute | solution.py:334
  32.6 11.0 %collective-permute-start.31 = (bf16[64,1280]{1,0:T(8,128)(2,1)S(1)}, bf16[64,1280]{1,0:T(8,128)(2,1)S(1)}, u32[]{:S(2)}, u32[]{:S(2)}) collective-permute-start(bf16[64,1280]{1,0:T(8,128)(2,1)S(1)} %get-tuple-element.85), channel_id=1, source_target_pairs={{0,3},{1,2},{2,1},{3,0},{4,7},{5,6},{6,5},{7,4},{8,11},{9,10},{10,... | collective-permute-start | bytes 491528 | tf_op jit(solution)/shard_map/ppermute | solution.py:334
  37.4 18.2 %collective-permute-start.6 = (bf16[96,1280]{1,0:T(8,128)(2,1)S(1)}, bf16[96,1280]{1,0:T(8,128)(2,1)S(1)}, u32[]{:S(2)}, u32[]{:S(2)}) collective-permute-start(bf16[96,1280]{1,0:T(8,128)(2,1)S(1)} %shard_map.119.refs_4_), channel_id=1, source_target_pairs={{0,8},{4,12},{8,0},{12,4},{16,24},{20,28},{24,16},{28,20},{1,9},{5... | collective-permute-start | bytes 737288 | tf_op jit(solution)/shard_map/ppermute | solution.py:329
  42.4 14.7 %collective-permute-start.7 = (bf16[96,1280]{1,0:T(8,128)(2,1)S(1)}, bf16[96,1280]{1,0:T(8,128)(2,1)S(1)}, u32[]{:S(2)}, u32[]{:S(2)}) collective-permute-start(bf16[96,1280]{1,0:T(8,128)(2,1)S(1)} %shard_map.119.refs_4_), channel_id=1, source_target_pairs={{0,16},{4,20},{8,24},{12,28},{16,0},{20,4},{24,8},{28,12},{1,17},{... | collective-permute-start | bytes 737288 | tf_op jit(solution)/shard_map/ppermute | solution.py:329
  43.6 11.1 %collective-permute-start.2 = (bf16[64,1280]{1,0:T(8,128)(2,1)S(1)}, bf16[64,1280]{1,0:T(8,128)(2,1)S(1)}, u32[]{:S(2)}, u32[]{:S(2)}) collective-permute-start(bf16[64,1280]{1,0:T(8,128)(2,1)S(1)} %collective-permute-done.refs_1_), channel_id=1, source_target_pairs={{0,16},{4,20},{8,24},{12,28},{16,0},{20,4},{24,8},{28,12},{1,17},{... | collective-permute-start | bytes 491528 | tf_op jit(solution)/shard_map/ppermute | solution.py:329
  54.7 8.0 %collective-permute-start.14 = (bf16[96,1280]{1,0:T(8,128)(2,1)S(1)}, bf16[96,1280]{1,0:T(8,128)(2,1)S(1)}, u32[]{:S(2)}, u32[]{:S(2)}) collective-permute-start(bf16[96,1280]{1,0:T(8,128)(2,1)S(1)} %shard_map.120.refs_4_), channel_id=1, source_target_pairs={{0,8},{4,12},{8,0},{12,4},{16,24},{20,28},{24,16},{28,20},{1,9},{5... | collective-permute-start | bytes 737288 | tf_op jit(solution)/shard_map/ppermute | solution.py:329
  55.6 8.8 %collective-permute-start.15 = (bf16[96,1280]{1,0:T(8,128)(2,1)S(1)}, bf16[96,1280]{1,0:T(8,128)(2,1)S(1)}, u32[]{:S(2)}, u32[]{:S(2)}) collective-permute-start(bf16[96,1280]{1,0:T(8,128)(2,1)S(1)} %shard_map.120.refs_4_), channel_id=1, source_target_pairs={{0,16},{4,20},{8,24},{12,28},{16,0},{20,4},{24,8},{28,12},{1,17},{... | collective-permute-start | bytes 737288 | tf_op jit(solution)/shard_map/ppermute | solution.py:329
  57.1 12.6 %collective-permute-start.33 = (bf16[96,1280]{1,0:T(8,128)(2,1)S(1)}, bf16[96,1280]{1,0:T(8,128)(2,1)S(1)}, u32[]{:S(2)}, u32[]{:S(2)}) collective-permute-start(bf16[96,1280]{1,0:T(8,128)(2,1)S(1)} %get-tuple-element.86.refs_4_.refs_12_), channel_id=1, source_target_pairs={{0,16},{4,20},{8,24},{12,28},{16,0},{20,4},{24,8},{28,12},{1,17},{... | collective-permute-start | bytes 737288 | tf_op jit(solution)/shard_map/ppermute | solution.py:329
  62.7 8.8 %collective-permute-start.35 = (bf16[96,1280]{1,0:T(8,128)(2,1)S(1)}, bf16[96,1280]{1,0:T(8,128)(2,1)S(1)}, u32[]{:S(2)}, u32[]{:S(2)}) collective-permute-start(bf16[96,1280]{1,0:T(8,128)(2,1)S(1)} %get-tuple-element.88.refs_4_.refs_12_), channel_id=1, source_target_pairs={{0,8},{4,12},{8,0},{12,4},{16,24},{20,28},{24,16},{28,20},{1,9},{5... | collective-permute-start | bytes 737288 | tf_op jit(solution)/shard_map/ppermute | solution.py:329
  64.4 11.6 %collective-permute-start.8 = (bf16[96,1280]{1,0:T(8,128)(2,1)S(1)}, bf16[96,1280]{1,0:T(8,128)(2,1)S(1)}, u32[]{:S(2)}, u32[]{:S(2)}) collective-permute-start(bf16[96,1280]{1,0:T(8,128)(2,1)S(1)} %collective-permute-done.7.refs_6_), channel_id=1, source_target_pairs={{0,8},{4,12},{8,0},{12,4},{16,24},{20,28},{24,16},{28,20},{1,9},{5... | collective-permute-start | bytes 737288 | tf_op jit(solution)/shard_map/ppermute | solution.py:329
  69.7 6.6 %collective-permute-start.16 = (bf16[96,1280]{1,0:T(8,128)(2,1)S(1)}, bf16[96,1280]{1,0:T(8,128)(2,1)S(1)}, u32[]{:S(2)}, u32[]{:S(2)}) collective-permute-start(bf16[96,1280]{1,0:T(8,128)(2,1)S(1)} %collective-permute-done.14.refs_5_), channel_id=1, source_target_pairs={{0,16},{4,20},{8,24},{12,28},{16,0},{20,4},{24,8},{28,12},{1,17},{... | collective-permute-start | bytes 737288 | tf_op jit(solution)/shard_map/ppermute | solution.py:329
  71.5 18.1 %collective-permute-start.36 = (bf16[96,1280]{1,0:T(8,128)(2,1)S(1)}, bf16[96,1280]{1,0:T(8,128)(2,1)S(1)}, u32[]{:S(2)}, u32[]{:S(2)}) collective-permute-start(bf16[96,1280]{1,0:T(8,128)(2,1)S(1)} %get-tuple-element.88.refs_4_.refs_12_), channel_id=1, source_target_pairs={{0,16},{4,20},{8,24},{12,28},{16,0},{20,4},{24,8},{28,12},{1,17},{... | collective-permute-start | bytes 737288 | tf_op jit(solution)/shard_map/ppermute | solution.py:329
  76.0 13.5 %collective-permute-start.28 = (bf16[64,1280]{1,0:T(8,128)(2,1)S(1)}, bf16[64,1280]{1,0:T(8,128)(2,1)S(1)}, u32[]{:S(2)}, u32[]{:S(2)}) collective-permute-start(bf16[64,1280]{1,0:T(8,128)(2,1)S(1)} %collective-permute-done.27.refs_2_.refs_10_), channel_id=1, source_target_pairs={{0,8},{4,12},{8,0},{12,4},{16,24},{20,28},{24,16},{28,20},{1,9},{5... | collective-permute-start | bytes 491528 | tf_op jit(solution)/shard_map/ppermute | solution.py:329
  76.3 13.3 %collective-permute-start.37 = (bf16[96,1280]{1,0:T(8,128)(2,1)S(1)}, bf16[96,1280]{1,0:T(8,128)(2,1)S(1)}, u32[]{:S(2)}, u32[]{:S(2)}) collective-permute-start(bf16[96,1280]{1,0:T(8,128)(2,1)S(1)} %collective-permute-done.35.refs_5_.refs_13_), channel_id=1, source_target_pairs={{0,16},{4,20},{8,24},{12,28},{16,0},{20,4},{24,8},{28,12},{1,17},{... | collective-permute-start | bytes 737288 | tf_op jit(solution)/shard_map/ppermute | solution.py:329
  78.7 14.4 %collective-permute-start.32 = (bf16[96,1280]{1,0:T(8,128)(2,1)S(1)}, bf16[96,1280]{1,0:T(8,128)(2,1)S(1)}, u32[]{:S(2)}, u32[]{:S(2)}) collective-permute-start(bf16[96,1280]{1,0:T(8,128)(2,1)S(1)} %get-tuple-element.86.refs_4_.refs_12_), channel_id=1, source_target_pairs={{0,8},{4,12},{8,0},{12,4},{16,24},{20,28},{24,16},{28,20},{1,9},{5... | collective-permute-start | bytes 737288 | tf_op jit(solution)/shard_map/ppermute | solution.py:329
  80.1 13.0 %collective-permute-start.34 = (bf16[96,1280]{1,0:T(8,128)(2,1)S(1)}, bf16[96,1280]{1,0:T(8,128)(2,1)S(1)}, u32[]{:S(2)}, u32[]{:S(2)}) collective-permute-start(bf16[96,1280]{1,0:T(8,128)(2,1)S(1)} %collective-permute-done.33.refs_6_.refs_14_), channel_id=1, source_target_pairs={{0,8},{4,12},{8,0},{12,4},{16,24},{20,28},{24,16},{28,20},{1,9},{5... | collective-permute-start | bytes 737288 | tf_op jit(solution)/shard_map/ppermute | solution.py:329
  89.5 13.9 %collective-permute-start.17 = (bf16[2,64,1280]{2,1,0:T(8,128)(2,1)S(1)}, bf16[2,64,1280]{2,1,0:T(8,128)(2,1)S(1)}, u32[]{:S(2)}, u32[]{:S(2)}) collective-permute-start(bf16[2,64,1280]{2,1,0:T(8,128)(2,1)S(1)} %get-tuple-element.70), channel_id=1, source_target_pairs={{0,16},{4,20},{8,24},{12,28},{16,0},{20,4},{24,8},{28,12},{1,17},{... | collective-permute-start | bytes 983048 | tf_op jit(solution)/shard_map/ppermute | solution.py:329
  96.6 8.2 %collective-permute-start.38 = (bf16[2,64,1280]{2,1,0:T(8,128)(2,1)S(1)}, bf16[2,64,1280]{2,1,0:T(8,128)(2,1)S(1)}, u32[]{:S(2)}, u32[]{:S(2)}) collective-permute-start(bf16[2,64,1280]{2,1,0:T(8,128)(2,1)S(1)} %get-tuple-element.93), channel_id=1, source_target_pairs={{0,8},{4,12},{8,0},{12,4},{16,24},{20,28},{24,16},{28,20},{1,9},{5... | collective-permute-start | bytes 983048 | tf_op jit(solution)/shard_map/ppermute | solution.py:329
  100.2 77.6 %collective-permute-start.50 = (bf16[2,320,1280]{2,1,0:T(8,128)(2,1)S(1)}, bf16[2,320,1280]{2,1,0:T(8,128)(2,1)S(1)}, u32[]{:S(2)}, u32[]{:S(2)}) collective-permute-start(bf16[2,320,1280]{2,1,0:T(8,128)(2,1)S(1)} %get-tuple-element.111), channel_id=1, source_target_pairs={{0,4},{4,0},{8,12},{12,8},{16,20},{20,16},{24,28},{28,24},{1,5},{5... | collective-permute-start | bytes 4915208 | tf_op jit(solution)/shard_map/ppermute | solution.py:329
  102.2 75.7 %collective-permute-start.51 = (bf16[2,320,1280]{2,1,0:T(8,128)(2,1)S(1)}, bf16[2,320,1280]{2,1,0:T(8,128)(2,1)S(1)}, u32[]{:S(2)}, u32[]{:S(2)}) collective-permute-start(bf16[2,320,1280]{2,1,0:T(8,128)(2,1)S(1)} %get-tuple-element.112), channel_id=1, source_target_pairs={{0,4},{4,0},{8,12},{12,8},{16,20},{20,16},{24,28},{28,24},{1,5},{5... | collective-permute-start | bytes 4915208 | tf_op jit(solution)/shard_map/ppermute | solution.py:329
  102.7 17.4 %collective-permute-start.40 = (bf16[2,96,1280]{2,1,0:T(8,128)(2,1)S(1)}, bf16[2,96,1280]{2,1,0:T(8,128)(2,1)S(1)}, u32[]{:S(2)}, u32[]{:S(2)}) collective-permute-start(bf16[2,96,1280]{2,1,0:T(8,128)(2,1)S(1)} %get-tuple-element.95), channel_id=1, source_target_pairs={{0,8},{4,12},{8,0},{12,4},{16,24},{20,28},{24,16},{28,20},{1,9},{5... | collective-permute-start | bytes 1474568 | tf_op jit(solution)/shard_map/ppermute | solution.py:329
  103.4 16.0 %collective-permute-start.18 = (bf16[1,64,1280]{2,1,0:T(8,128)(2,1)S(1)}, bf16[1,64,1280]{2,1,0:T(8,128)(2,1)S(1)}, u32[]{:S(2)}, u32[]{:S(2)}) collective-permute-start(bf16[1,64,1280]{2,1,0:T(8,128)(2,1)S(1)} %shard_map.123), channel_id=1, source_target_pairs={{0,8},{4,12},{8,0},{12,4},{16,24},{20,28},{24,16},{28,20},{1,9},{5... | collective-permute-start | bytes 491528 | tf_op jit(solution)/shard_map/ppermute | solution.py:329
  104.9 17.3 %collective-permute-start.43 = (bf16[2,96,1280]{2,1,0:T(8,128)(2,1)S(1)}, bf16[2,96,1280]{2,1,0:T(8,128)(2,1)S(1)}, u32[]{:S(2)}, u32[]{:S(2)}) collective-permute-start(bf16[2,96,1280]{2,1,0:T(8,128)(2,1)S(1)} %get-tuple-element.98), channel_id=1, source_target_pairs={{0,16},{4,20},{8,24},{12,28},{16,0},{20,4},{24,8},{28,12},{1,17},{... | collective-permute-start | bytes 1474568 | tf_op jit(solution)/shard_map/ppermute | solution.py:329
  119.4 12.3 %collective-permute-start.19 = (bf16[2,96,1280]{2,1,0:T(8,128)(2,1)S(1)}, bf16[2,96,1280]{2,1,0:T(8,128)(2,1)S(1)}, u32[]{:S(2)}, u32[]{:S(2)}) collective-permute-start(bf16[2,96,1280]{2,1,0:T(8,128)(2,1)S(1)} %get-tuple-element.72), channel_id=1, source_target_pairs={{0,8},{4,12},{8,0},{12,4},{16,24},{20,28},{24,16},{28,20},{1,9},{5... | collective-permute-start | bytes 1474568 | tf_op jit(solution)/shard_map/ppermute | solution.py:329
  120.1 14.1 %collective-permute-start.21 = (bf16[2,96,1280]{2,1,0:T(8,128)(2,1)S(1)}, bf16[2,96,1280]{2,1,0:T(8,128)(2,1)S(1)}, u32[]{:S(2)}, u32[]{:S(2)}) collective-permute-start(bf16[2,96,1280]{2,1,0:T(8,128)(2,1)S(1)} %get-tuple-element.74), channel_id=1, source_target_pairs={{0,16},{4,20},{8,24},{12,28},{16,0},{20,4},{24,8},{28,12},{1,17},{... | collective-permute-start | bytes 1474568 | tf_op jit(solution)/shard_map/ppermute | solution.py:329
  122.2 17.3 %collective-permute-start.41 = (bf16[1,96,1280]{2,1,0:T(8,128)(2,1)S(1)}, bf16[1,96,1280]{2,1,0:T(8,128)(2,1)S(1)}, u32[]{:S(2)}, u32[]{:S(2)}) collective-permute-start(bf16[1,96,1280]{2,1,0:T(8,128)(2,1)S(1)} %shard_map.132), channel_id=1, source_target_pairs={{0,16},{4,20},{8,24},{12,28},{16,0},{20,4},{24,8},{28,12},{1,17},{... | collective-permute-start | bytes 737288 | tf_op jit(solution)/shard_map/ppermute | solution.py:329
  131.8 9.1 %collective-permute-start.44 = (bf16[1,96,1280]{2,1,0:T(8,128)(2,1)S(1)}, bf16[1,96,1280]{2,1,0:T(8,128)(2,1)S(1)}, u32[]{:S(2)}, u32[]{:S(2)}) collective-permute-start(bf16[1,96,1280]{2,1,0:T(8,128)(2,1)S(1)} %shard_map.134), channel_id=1, source_target_pairs={{0,8},{4,12},{8,0},{12,4},{16,24},{20,28},{24,16},{28,20},{1,9},{5... | collective-permute-start | bytes 737288 | tf_op jit(solution)/shard_map/ppermute | solution.py:329
  134.2 12.3 %collective-permute-start.20 = (bf16[1,96,1280]{2,1,0:T(8,128)(2,1)S(1)}, bf16[1,96,1280]{2,1,0:T(8,128)(2,1)S(1)}, u32[]{:S(2)}, u32[]{:S(2)}) collective-permute-start(bf16[1,96,1280]{2,1,0:T(8,128)(2,1)S(1)} %shard_map.124), channel_id=1, source_target_pairs={{0,16},{4,20},{8,24},{12,28},{16,0},{20,4},{24,8},{28,12},{1,17},{... | collective-permute-start | bytes 737288 | tf_op jit(solution)/shard_map/ppermute | solution.py:329
  139.5 9.0 %collective-permute-start.22 = (bf16[1,96,1280]{2,1,0:T(8,128)(2,1)S(1)}, bf16[1,96,1280]{2,1,0:T(8,128)(2,1)S(1)}, u32[]{:S(2)}, u32[]{:S(2)}) collective-permute-start(bf16[1,96,1280]{2,1,0:T(8,128)(2,1)S(1)} %shard_map.125), channel_id=1, source_target_pairs={{0,8},{4,12},{8,0},{12,4},{16,24},{20,28},{24,16},{28,20},{1,9},{5... | collective-permute-start | bytes 737288 | tf_op jit(solution)/shard_map/ppermute | solution.py:329
  146.5 6.9 %collective-permute-start.45 = (bf16[32,1280]{1,0:T(8,128)(2,1)S(1)}, bf16[32,1280]{1,0:T(8,128)(2,1)S(1)}, u32[]{:S(2)}, u32[]{:S(2)}) collective-permute-start(bf16[32,1280]{1,0:T(8,128)(2,1)S(1)} %get-tuple-element.99), channel_id=1, source_target_pairs={{0,1},{1,0},{2,3},{3,2},{4,5},{5,4},{6,7},{7,6},{8,9},{9,8},{10,11... | collective-permute-start | bytes 245768 | tf_op jit(solution)/shard_map/ppermute | solution.py:334
  148.5 10.3 %collective-permute-start.46 = (bf16[32,1280]{1,0:T(8,128)(2,1)S(1)}, bf16[32,1280]{1,0:T(8,128)(2,1)S(1)}, u32[]{:S(2)}, u32[]{:S(2)}) collective-permute-start(bf16[32,1280]{1,0:T(8,128)(2,1)S(1)} %get-tuple-element.100), channel_id=1, source_target_pairs={{0,2},{1,3},{2,0},{3,1},{4,6},{5,7},{6,4},{7,5},{8,10},{9,11},{10,... | collective-permute-start | bytes 245768 | tf_op jit(solution)/shard_map/ppermute | solution.py:334
  151.5 9.9 %collective-permute-start.47 = (bf16[32,1280]{1,0:T(8,128)(2,1)S(1)}, bf16[32,1280]{1,0:T(8,128)(2,1)S(1)}, u32[]{:S(2)}, u32[]{:S(2)}) collective-permute-start(bf16[32,1280]{1,0:T(8,128)(2,1)S(1)} %get-tuple-element.101), channel_id=1, source_target_pairs={{0,2},{1,3},{2,0},{3,1},{4,6},{5,7},{6,4},{7,5},{8,10},{9,11},{10,... | collective-permute-start | bytes 245768 | tf_op jit(solution)/shard_map/ppermute | solution.py:334
  153.4 8.1 %collective-permute-start.48 = (bf16[32,1280]{1,0:T(8,128)(2,1)S(1)}, bf16[32,1280]{1,0:T(8,128)(2,1)S(1)}, u32[]{:S(2)}, u32[]{:S(2)}) collective-permute-start(bf16[32,1280]{1,0:T(8,128)(2,1)S(1)} %get-tuple-element.102), channel_id=1, source_target_pairs={{0,3},{1,2},{2,1},{3,0},{4,7},{5,6},{6,5},{7,4},{8,11},{9,10},{10,... | collective-permute-start | bytes 245768 | tf_op jit(solution)/shard_map/ppermute | solution.py:334
  158.8 8.7 %collective-permute-start.49 = (bf16[32,1280]{1,0:T(8,128)(2,1)S(1)}, bf16[32,1280]{1,0:T(8,128)(2,1)S(1)}, u32[]{:S(2)}, u32[]{:S(2)}) collective-permute-start(bf16[32,1280]{1,0:T(8,128)(2,1)S(1)} %get-tuple-element.103), channel_id=1, source_target_pairs={{0,3},{1,2},{2,1},{3,0},{4,7},{5,6},{6,5},{7,4},{8,11},{9,10},{10,... | collective-permute-start | bytes 245768 | tf_op jit(solution)/shard_map/ppermute | solution.py:334
  161.5 9.3 %collective-permute-start.23 = (bf16[64,1280]{1,0:T(8,128)(2,1)S(1)}, bf16[64,1280]{1,0:T(8,128)(2,1)S(1)}, u32[]{:S(2)}, u32[]{:S(2)}) collective-permute-start(bf16[64,1280]{1,0:T(8,128)(2,1)S(1)} %get-tuple-element.75), channel_id=1, source_target_pairs={{0,1},{1,0},{2,3},{3,2},{4,5},{5,4},{6,7},{7,6},{8,9},{9,8},{10,11... | collective-permute-start | bytes 491528 | tf_op jit(solution)/shard_map/ppermute | solution.py:334
  161.5 14.9 %collective-permute-start.24 = (bf16[64,1280]{1,0:T(8,128)(2,1)S(1)}, bf16[64,1280]{1,0:T(8,128)(2,1)S(1)}, u32[]{:S(2)}, u32[]{:S(2)}) collective-permute-start(bf16[64,1280]{1,0:T(8,128)(2,1)S(1)} %get-tuple-element.76), channel_id=1, source_target_pairs={{0,2},{1,3},{2,0},{3,1},{4,6},{5,7},{6,4},{7,5},{8,10},{9,11},{10,... | collective-permute-start | bytes 491528 | tf_op jit(solution)/shard_map/ppermute | solution.py:334
  167.6 8.8 %collective-permute-start.25 = (bf16[64,1280]{1,0:T(8,128)(2,1)S(1)}, bf16[64,1280]{1,0:T(8,128)(2,1)S(1)}, u32[]{:S(2)}, u32[]{:S(2)}) collective-permute-start(bf16[64,1280]{1,0:T(8,128)(2,1)S(1)} %get-tuple-element.77), channel_id=1, source_target_pairs={{0,3},{1,2},{2,1},{3,0},{4,7},{5,6},{6,5},{7,4},{8,11},{9,10},{10,... | collective-permute-start | bytes 491528 | tf_op jit(solution)/shard_map/ppermute | solution.py:334
  (9 other events, 158.6 us)
